TPU v7x, 256 devices: a whole 4x4x8 slice. The times are simulated.
256 devices in a mesh: gx: 32 (over z, x), st: 8 (over y, core).
Axes of the slice: x: 4, y: 4, z: 8, core: 2. Of those that a mesh axis runs over, the one named last changes fastest.
Arguments:
- checkpoint: float32 [26, 256, 64, 128], P(None, ('gx', 'st')), may hold values from -0.5 to 1, as said below
- adjoint_in: float32 [26, 256, 64, 128], P(None, 'gx', 'st'), may hold values from -6 to 6
- solid_mask: int32 [256, 64, 128], P('gx', 'st'), may hold values 0 or 1
- tile_map: int32 [256, 64], P('gx', 'st'), may hold values from 0 to 4095
- theta: float32 [4096], replicated, may hold values from 0.8 to 1.2
- first_moment: float32 [4096], replicated, may hold values from -6 to 6
- second_moment: float32 [4096], replicated, may hold values from 1 to 30
Outputs:
- adjoint_out: float32 [26, 256, 64, 128], P(None, 'gx', 'st')
- theta_new: float32 [4096], replicated
- first_new: float32 [4096], replicated
- second_new: float32 [4096], replicated
- nusselt: float32 [], replicated
Inputs may be any that keep to these rules, and one draw needn't show every extreme that they name: `checkpoint`: populations near a local equilibrium; the flow populations of a cell sum to a density near 1.
All inputs are finite; a program needn't handle non-finite values. No bound on the sum of `solid_mask` on one device may be relied on, other than what follows from the above.
Results may differ from a plain program's by a relative error of at most 0.0001.
Values sent between devices are 32-bit elements; how exact they have to be, the bound alone decides.
No kernel may reach another device: no remote copies, remote signals or barrier semaphores. Data moves between devices by JAX's collectives and lax.ppermute only.
A program may use at most 64 MiB of HBM per device.

v0:
```python
import jax
import jax.numpy as jnp
import numpy as np
from jax import lax
from jax.experimental import pallas as pl
from jax.experimental.pallas import tpu as pltpu
from jax.sharding import PartitionSpec as P


ADAM_STEP = 100

VELOCITY = np.array(
    [
        [0, 0, 0],
        [1, 0, 0],
        [-1, 0, 0],
        [0, 1, 0],
        [0, -1, 0],
        [0, 0, 1],
        [0, 0, -1],
        [1, 1, 0],
        [-1, -1, 0],
        [1, -1, 0],
        [-1, 1, 0],
        [1, 0, 1],
        [-1, 0, -1],
        [1, 0, -1],
        [-1, 0, 1],
        [0, 1, 1],
        [0, -1, -1],
        [0, 1, -1],
        [0, -1, 1],
        [0, 0, 0],
        [1, 0, 0],
        [-1, 0, 0],
        [0, 1, 0],
        [0, -1, 0],
        [0, 0, 1],
        [0, 0, -1],
    ],
    dtype=np.int32,
)
VEL = [tuple(int(v) for v in row) for row in VELOCITY]
OPP = [0, 2, 1, 4, 3, 6, 5, 8, 7, 10, 9, 12, 11, 14, 13, 16, 15, 18, 17, 19, 21, 20, 23, 22, 25, 24]
FLOW_PAIRS = [(i, i + 1) for i in range(1, 19, 2)]
HEAT_PAIRS = [(20, 21), (22, 23), (24, 25)]
INV_TAU = 1.25
KEEP = 1.0 - INV_TAU
LIFT = 0.8 * 0.001
MEAN_TEMP = 0.5
KAPPA = 0.075
RISING = 24
LEARN_RATE = 0.05
BETA_ONE = 0.9
BETA_TWO = 0.99
ADAM_EPS = 1e-08

HALO = 4
OWN = 8
WIDE = OWN + 2 * HALO
DEPTH = 128
INTERPRET = False


def weight(i):
    if i < 19:
        return 1.0 / 3.0 if i == 0 else (1.0 / 18.0 if i < 7 else 1.0 / 36.0)
    return 0.25 if i == 19 else 0.125


def call(kernel, outs, scratch=(), mib=8, scalars=0, inputs=None, out_specs=None, in_specs=None):
    extra = {}
    if in_specs:
        extra["in_specs"] = [pl.BlockSpec(memory_space=space) for space in in_specs]
    if scalars:
        extra["in_specs"] = [pl.BlockSpec(memory_space=pltpu.SMEM)] * scalars + [
            pl.BlockSpec(memory_space=pltpu.VMEM)
        ] * (inputs - scalars)
    if out_specs:
        extra["out_specs"] = [pl.BlockSpec(memory_space=space) for space in out_specs]
    return pl.pallas_call(
        kernel,
        out_shape=[jax.ShapeDtypeStruct(s, jnp.float32) for s in outs],
        scratch_shapes=list(scratch),
        compiler_params=pltpu.CompilerParams(vmem_limit_bytes=mib << 20),
        interpret=INTERPRET,
        **extra,
    )


class At:
    def __init__(self, index, offset):
        self.index, self.offset = index, offset

    def by(self, more):
        return self.index + (self.offset + more) if self.offset + more else self.index


def loop(count, fn):
    lax.fori_loop(0, count, lambda i, c: (fn(i), c)[1], 0)


def shifted(value, step_y, step_z):
    if step_y:
        value = pltpu.roll(value, step_y % value.shape[0], 0)
    if step_z:
        value = pltpu.roll(value, step_z % DEPTH, 1)
    return value


def lane_is(k, rows=WIDE):
    return lax.broadcasted_iota(jnp.int32, (rows, DEPTH), 1) == k


def table_of(i):
    if i >= 24:
        return i - 6
    if i >= 19:
        return i - 20
    return i - 1


def add_all(values):
    total = values[0]
    for value in values[1:]:
        total = total + value
    return total


def signed_sum(terms):
    total = None
    for sign, value in terms:
        if total is None:
            total = value if sign > 0 else -value
        else:
            total = total + value if sign > 0 else total - value
    return total


def moments(s):
    diff = {}
    parts = [s[0]]
    for i, j in FLOW_PAIRS:
        parts.append(s[i] + s[j])
        diff[i] = s[i] - s[j]
    density = add_all(parts)
    speed = []
    for axis in range(3):
        speed.append(signed_sum([(VEL[i][axis], diff[i]) for i, _ in FLOW_PAIRS if VEL[i][axis]]))
    temper = add_all([s[i] for i in range(19, 26)])
    return density, speed, temper


def collided(s, density, speed, temper):
    ux, uy, uz = speed
    vz = uz + LIFT * (temper - MEAN_TEMP)
    vel = (ux, uy, vz)
    base = density - 1.5 * (ux * ux + uy * uy + vz * vz)
    out = [None] * 26
    out[0] = KEEP * s[0] + (INV_TAU * weight(0)) * base
    for i, j in FLOW_PAIRS:
        proj = signed_sum([(VEL[i][a], vel[a]) for a in range(3) if VEL[i][a]])
        factor = INV_TAU * weight(i)
        even = factor * base + (4.5 * factor) * (proj * proj)
        odd = (3.0 * factor) * proj
        out[i] = KEEP * s[i] + (even + odd)
        out[j] = KEEP * s[j] + (even - odd)
    out[19] = KEEP * s[19] + (INV_TAU * weight(19)) * temper
    scaled = (INV_TAU * weight(20)) * temper
    for (i, j), u in zip(HEAT_PAIRS, (ux, uy, uz)):
        odd = scaled * (4.0 * u)
        out[i] = KEEP * s[i] + (scaled + odd)
        out[j] = KEEP * s[j] + (scaled - odd)
    return out


LINES = 26 * WIDE
FLAG_LINES = 2 * OWN * 4
PLANE_FLAGS = 2 * HALO * WIDE


def fill_tall(plane, tall):
    def fill(c):
        tall[c, 0:4] = plane[c, 60:64]
        tall[c, 4:68] = plane[c]
        tall[c, 68:72] = plane[c, 0:4]

    loop(26, fill)


def copy_slot(place, tall, k, out):
    base = pl.multiple_of(OWN * lax.rem(place[0] + k, 8), 8)

    def one(c):
        out[pl.ds(pl.multiple_of(WIDE * c, WIDE), WIDE)] = tall[c, pl.ds(base, WIDE)]

    loop(26, one)


def pack_kernel(place, plane, *refs):
    outs, tall = refs[:6], refs[6]
    fill_tall(plane, tall)
    for k, out in zip((0, 2, 3, 4, 5, 6), outs):
        copy_slot(place, tall, k, out)


def pack_flags_kernel(place, plane, flags, up, down, tall):
    fill_tall(plane, tall)
    copy_slot(place, tall, 1, up)
    copy_slot(place, tall, 7, down)
    for f in range(2):
        for x in range(OWN):
            at = LINES + 4 * (OWN * f + x)
            up[at : at + 4] = flags[f, x, 4:8]
            down[at : at + 4] = flags[f, x, 0:4]


def tall_flags(flags, low, high, f, x):
    at = LINES + 4 * (OWN * f + x)
    return ((0, 4, low[at : at + 4]), (4, 12, flags[f, x]), (12, 16, high[at : at + 4]))


def route_kernel(place, pairs, refs, plus, minus):
    for q, k in enumerate(pairs):
        n = lax.rem(place[0] + (8 - k), 8)
        one, two = refs[2 * q], refs[2 * q + 1]

        def move(first, second, q=q):
            def step(c):
                there = pl.ds(pl.multiple_of(32 * c, 32), 32)
                to = pl.ds(pl.multiple_of(32 * c + LINES * q, 32), 32)
                plus[to] = first[there]
                minus[to] = second[there]

            loop(LINES // 32, step)

        @pl.when(n >= HALO)
        def _(move=move, one=one, two=two):
            move(one, two)

        @pl.when(n < HALO)
        def _(move=move, one=one, two=two):
            move(two, one)


FIRST, SECOND = (1, 3), (0, 2)


def route_first_kernel(place, a, b, c, d, flags, plus, minus):
    route_kernel(place, FIRST, (a, b, c, d), plus, minus)
    low, high = a, d
    for f in range(2):
        for n in range(HALO):
            at = 2 * LINES + WIDE * (HALO * f + n)
            for lo, hi, value in tall_flags(flags, low, high, f, n + HALO):
                plus[at + lo : at + hi] = value
            for lo, hi, value in tall_flags(flags, low, high, f, n):
                minus[at + lo : at + hi] = value


def route_second_kernel(place, a, b, c, d, plus, minus):
    route_kernel(place, SECOND, (a, b, c, d), plus, minus)


def table_kernel(low, high, flags, from_left, from_right, region, table):
    for f in range(2):
        for x in range(OWN):
            for lo, hi, value in tall_flags(flags, low, high, f, x):
                region[f, x + HALO, lo:hi] = value
        for n in range(HALO):
            at = 2 * LINES + WIDE * (HALO * f + n)
            region[f, n] = from_left[at : at + WIDE]
            region[f, n + HALO + OWN] = from_right[at : at + WIDE]
    first = lane_is(0)
    last = lane_is(DEPTH - 1)

    def one(n):
        at = At(n, 1)
        x = at.by(0)
        for i in range(1, 19):
            cx, cy, cz = VEL[i]
            value = shifted(region[0, at.by(-cx)], cy, cz)
            if cz:
                edge = first if cz > 0 else last
                if i in (5, 6):
                    table[x, table_of(i + 19)] = jnp.where(edge, -1.0, value)
                value = jnp.where(edge, 1.0, value)
            table[x, table_of(i)] = value

    loop(WIDE - 2, one)


def streamed(p, table, at):
    x = at.by(0)
    s = []
    for i in range(26):
        if i in (0, 19):
            s.append(p[x, i])
            continue
        cx, cy, cz = VEL[i]
        moved = shifted(p[at.by(-cx), i], cy, cz)
        t = table[x, table_of(i)]
        back = p[x, OPP[i]]
        if i >= 24:
            back = t * back
        s.append(jnp.where(t == 0.0, moved, back))
    return s


def forward_kernel(place, *refs):
    planes, halos = refs[:8], refs[8:12]
    table, region, mom, edge, edge_lo, edge_hi, heat, pa, pb, mom3 = refs[12:]
    first = lane_is(0)

    def start(src, x, off=0):
        s = [src[off + WIDE * i : off + WIDE * (i + 1)] for i in range(26)]
        density, speed, temper = moments(s)
        for a, value in enumerate((*speed, temper)):
            mom[0, x, a] = value
        for i, value in enumerate(collided(s, density, speed, temper)):
            pa[x, i] = value

    for k in range(8):
        n = lax.rem(place[0] + (8 - k), 8)
        start(planes[k], n + HALO)
    for group, pairs in enumerate((FIRST, SECOND)):
        for q, k in enumerate(pairs):
            n = lax.rem(place[0] + (8 - k), HALO)
            start(halos[2 * group], n, LINES * q)
            start(halos[2 * group + 1], n + OWN + HALO, LINES * q)

    def arrive(p, at):
        s = streamed(p, table, at)
        s[RISING] = s[RISING] + jnp.where(first, 0.25 * region[1, at.by(0)], 0.0)
        return s

    src, dst = pa, pb
    for k in range(1, 4):

        def one(n, k=k, src=src, dst=dst):
            at = At(n, k)
            x = at.by(0)
            s = arrive(src, at)
            density, speed, temper = moments(s)
            for a, value in enumerate((*speed, temper)):
                if k < 3:
                    mom[k, x, a] = value
                else:
                    mom3[x, a] = value
            for i, value in enumerate(collided(s, density, speed, temper)):
                dst[x, i] = value

        loop(WIDE - 2 * k, one)
        src, dst = dst, src

    def last(n, total):
        at = At(n, HALO)
        x = at.by(0)
        s = arrive(src, at)
        _, speed, temper = moments(s)
        values = [mom3[x, a] for a in range(4)] + [speed[2], temper]
        for a, value in enumerate(values):
            edge[n, a] = value[4:12]
            edge_lo[n, a] = value[4:8]
            edge_hi[n, a] = value[8:12]
        flux = (1.0 - region[0, x]) * speed[2] * temper
        return total + flux[4:12]

    total = lax.fori_loop(0, OWN, last, jnp.zeros((OWN, DEPTH), jnp.float32))
    heat[...] = jnp.broadcast_to(jnp.sum(total), heat.shape)


def adjoint_cell(lam, table, at, fluids, vel, temper):
    x = at.by(0)
    fluid, fluid_up, fluid_down = fluids
    ux, uy, uz = vel
    vz = uz + LIFT * (temper - MEAN_TEMP)
    v = (ux, uy, vz)

    def mu_of(j):
        cx, cy, cz = VEL[j]
        if j in (0, 19):
            return lam[x, j]
        moved = shifted(lam[at.by(cx), j], -cy, -cz)
        keep = fluid if cz == 0 else (fluid_up if cz > 0 else fluid_down)
        return keep * moved + table[x, table_of(OPP[j])] * lam[x, OPP[j]]

    mu = [mu_of(j) for j in range(26)]
    axis_sum = add_all([mu[i] + mu[j] for i, j in FLOW_PAIRS[:3]])
    pair_sum = {i: mu[i] + mu[j] for i, j in FLOW_PAIRS}
    pair_diff = {i: mu[i] - mu[j] for i, j in FLOW_PAIRS}
    wa, wd = weight(1), weight(7)
    diag = add_all([pair_sum[i] for i, _ in FLOW_PAIRS[3:]])
    zeroth = weight(0) * mu[0] + wa * axis_sum + wd * diag

    def first(a):
        axis = 1 + 2 * a
        rest = signed_sum([(VEL[i][a], pair_diff[i]) for i, _ in FLOW_PAIRS[3:] if VEL[i][a]])
        return wa * pair_diff[axis] + wd * rest

    def second(a, b):
        if a == b:
            rest = add_all([pair_sum[i] for i, _ in FLOW_PAIRS[3:] if VEL[i][a]])
            return wa * pair_sum[1 + 2 * a] + wd * rest
        return wd * signed_sum(
            [(VEL[i][a] * VEL[i][b], pair_sum[i]) for i, _ in FLOW_PAIRS[3:] if VEL[i][a] * VEL[i][b]]
        )

    m2 = {(a, b): second(a, b) for a in range(3) for b in range(a, 3)}
    force = []
    for a in range(3):
        bent = add_all([m2[min(a, b), max(a, b)] * v[b] for b in range(3)])
        force.append(3.0 * first(a) + 9.0 * bent - 3.0 * (v[a] * zeroth))
    heat_diff = [mu[i] - mu[j] for i, j in HEAT_PAIRS]
    heat_even = weight(19) * mu[19] + weight(20) * add_all([mu[i] + mu[j] for i, j in HEAT_PAIRS])
    wh = 4.0 * weight(20)
    heat_odd = add_all([heat_diff[a] * (wh * u) for a, u in enumerate((ux, uy, uz))])
    to_heat = INV_TAU * (LIFT * force[2] + heat_even + heat_odd)
    scaled = wh * temper
    pull = [INV_TAU * (force[a] + scaled * heat_diff[a]) for a in range(3)]
    base = INV_TAU * zeroth
    out = [None] * 26
    out[0] = KEEP * mu[0] + base
    for i, j in FLOW_PAIRS:
        proj = signed_sum([(VEL[i][a], pull[a]) for a in range(3) if VEL[i][a]])
        out[i] = KEEP * mu[i] + (base + proj)
        out[j] = KEEP * mu[j] + (base - proj)
    for i in range(19, 26):
        out[i] = KEEP * mu[i] + to_heat
    return out


def merge_kernel(lo, mid, hi, head, tail):
    for n in range(HALO):
        for out, x in ((head, n), (tail, n + HALO)):
            for a in range(6):
                out[n, a, 0:4] = lo[x, a]
                out[n, a, 4:12] = mid[x, a]
                out[n, a, 12:16] = hi[x, a]


def adjoint_planes(k, state_of, bufs, table, region, put):
    first = lane_is(0)
    last = lane_is(DEPTH - 1)

    def one(n):
        at = At(n, HALO - k)
        x = at.by(0)
        fluid = 1.0 - region[0, x]
        fluids = (fluid, jnp.where(last, 0.0, fluid), jnp.where(first, 0.0, fluid))
        state = [state_of(x, a) for a in range(4)]
        for chain, src in enumerate(bufs):
            lam = adjoint_cell(src, table, at, fluids, state[:3], state[3])
            for i in range(26):
                put(chain, n, x, i, lam[i])

    loop(OWN + 2 * k, one)


def backward_kernel(*refs):
    own, gl, gr, slo, shi, elo, emid, ehi, el, er, mom, table, region, names, heat = refs[:15]
    out_a, out_b, slots, la0, la1, lb0, lb1, late, sums, last_a, last_b, sems = refs[15:]

    def gather(src, count, off):
        def one(x):
            for i in range(26):
                la0[x + off, i, 0:4] = slo[i, x + off]
                la0[x + off, i, 4:12] = src[i, x]
                la0[x + off, i, 12:16] = shi[i, x + off]

        loop(count, one)

    gather(gl, HALO, 0)
    gather(own, OWN, HALO)
    gather(gr, HALO, HALO + OWN)

    def settle(x):
        for a in range(6):
            late[x + HALO, a, 0:4] = elo[x, a]
            late[x + HALO, a, 4:12] = emid[x, a]
            late[x + HALO, a, 12:16] = ehi[x, a]

    loop(OWN, settle)

    def flank(x):
        for a in range(6):
            late[x, a] = el[x, a]
            late[x + HALO + OWN, a] = er[x, a]

    loop(HALO, flank)

    def seed(x):
        fluid = 1.0 - region[0, x]
        up = fluid * late[x, 5]
        zero = jnp.zeros_like(up)
        heat = fluid * late[x, 4]
        for i in range(26):
            cz = VEL[i][2]
            lb0[x, i] = heat if i >= 19 else (zero if cz == 0 else (up if cz > 0 else -up))

    loop(WIDE, seed)

    def collect(chain, lam, fresh):
        for n in range(OWN):
            value = lam[n + HALO, RISING][4:12]
            spot = pl.ds(OWN * OWN * chain + OWN * n, OWN)
            sums[spot] = value if fresh else sums[spot] + value

    bufs = [(la0, la1), (lb0, lb1)]
    for k in (3, 2, 1, 0):
        for chain, (src, _) in enumerate(bufs):
            collect(chain, src, k == 3)

        def put(chain, n, x, i, value, k=k, dsts=(bufs[0][1], bufs[1][1])):
            if k == 0:
                (last_a, last_b)[chain][i, n] = value[4:12]
            else:
                dsts[chain][x, i] = value

        def state_of(x, a, k=k):
            return late[x, a] if k == 3 else mom[k, x, a]

        adjoint_planes(k, state_of, [src for src, _ in bufs], table, region, put)
        bufs = [(dst, src) for src, dst in bufs]
    copies = [
        pltpu.make_async_copy(last_a, out_a, sems.at[0]),
        pltpu.make_async_copy(last_b, out_b, sems.at[1]),
    ]
    for copy in copies:
        copy.start()

    line = 0.25 * jnp.transpose(sums[...])[0:1]
    lane = lax.broadcasted_iota(jnp.int32, (1, DEPTH), 1)
    pair = jnp.concatenate([line, jnp.where(lane < OWN * OWN, names[...], heat[...])], 0)
    count = slots.shape[0]

    def spread(n):
        for q in range(8):
            slots[8 * n + q] = pair

    loop(count // 8, spread)
    for copy in copies:
        copy.wait()


def split3(value):
    high = value.astype(jnp.bfloat16)
    rest = value - high.astype(jnp.float32)
    mid = rest.astype(jnp.bfloat16)
    low = (rest - mid.astype(jnp.float32)).astype(jnp.bfloat16)
    return high, mid, low


def tile_kernel(
    scale, told, theta, first, second, part_a, part_b, theta_new, first_new, second_new, nusselt, adjoint, va, vb, sems
):
    copies = [
        pltpu.make_async_copy(part_a, va, sems.at[0]),
        pltpu.make_async_copy(part_b, vb, sems.at[1]),
    ]
    for copy in copies:
        copy.start()
    rows = told.shape[0] // 2
    half = DEPTH // 2
    lane = lax.broadcasted_iota(jnp.int32, (8, DEPTH), 1)
    left = lane < half

    def flux(r, total):
        return total + told[pl.ds(pl.multiple_of(8 * r, 8), 8)]

    total = lax.fori_loop(0, rows // 4, flux, jnp.zeros((8, DEPTH), jnp.float32), unroll=8)
    odd = lax.rem(lax.broadcasted_iota(jnp.int32, (8, DEPTH), 0), 2) == 1
    share = jnp.sum(jnp.where(odd & (lane == half), total, 0.0)) * scale[0]
    nusselt[0, 0] = 1.0 + share

    def one(r, total):
        base = pl.multiple_of(32 * r, 32)
        even_grad = told[pl.ds(base, 8, stride=4)]
        even_name = told[pl.ds(base + 1, 8, stride=4)]
        odd_grad = told[pl.ds(base + 2, 8, stride=4)]
        odd_name = told[pl.ds(base + 3, 8, stride=4)]

        def whole(pair):
            return pair + share * pltpu.roll(pair, half, 1)

        value = jnp.where(left, whole(even_grad), pltpu.roll(whole(odd_grad), half, 1))
        ident = jnp.where(left, even_name, pltpu.roll(odd_name, half, 1)).astype(jnp.int32)
        upper = ident // DEPTH
        lower = ident - upper * DEPTH
        pieces = [piece.astype(jnp.float32) for piece in split3(value)]
        high_is = lax.broadcasted_iota(jnp.int32, (32, DEPTH), 0)
        low_is = lax.broadcasted_iota(jnp.int32, (DEPTH, DEPTH), 0)
        lhs, rhs = [], []
        for q in range(8):
            hot = high_is == jnp.broadcast_to(upper[q : q + 1], (32, DEPTH))
            lhs.append(
                jnp.concatenate(
                    [
                        jnp.where(hot, jnp.broadcast_to(piece[q : q + 1], (32, DEPTH)), 0.0)
                        for piece in pieces
                    ],
                    0,
                ).astype(jnp.bfloat16)
            )
            hot = low_is == jnp.broadcast_to(lower[q : q + 1], (DEPTH, DEPTH))
            rhs.append(jnp.where(hot, 1.0, 0.0).astype(jnp.bfloat16))
        return total + lax.dot_general(
            jnp.concatenate(lhs, 1),
            jnp.concatenate(rhs, 1),
            (((1,), (1,)), ((), ())),
            preferred_element_type=jnp.float32,
        )

    total = lax.fori_loop(0, rows // 16, one, jnp.zeros((96, DEPTH), jnp.float32), unroll=2)
    grad = (total[0:32] + total[32:64]) + total[64:96]
    new_first = BETA_ONE * first[...] + (1.0 - BETA_ONE) * grad
    new_second = BETA_TWO * second[...] + (1.0 - BETA_TWO) * grad * grad
    first_hat = new_first / (1.0 - BETA_ONE**ADAM_STEP)
    second_hat = new_second / (1.0 - BETA_TWO**ADAM_STEP)
    theta_new[...] = theta[...] - LEARN_RATE * first_hat / (jnp.sqrt(second_hat) + ADAM_EPS)
    first_new[...] = new_first
    second_new[...] = new_second
    for copy in copies:
        copy.wait()

    def combine(c):
        adjoint[c] = va[c] + share * vb[c]

    loop(26, combine)


def neighbour(value, axis, step):
    count = lax.axis_size(axis)
    return lax.ppermute(value, axis, [(i, (i + step) % count) for i in range(count)])


def after(value, *earlier):
    return lax.optimization_barrier((value, *earlier))[0]


def window(checkpoint, adjoint_in, solid_mask, tile_map, theta, first_moment, second_moment):
    vmem = pltpu.VMEM
    f32 = jnp.float32
    place = lax.axis_index("st").astype(jnp.int32).reshape(1)
    smem, on_chip = [pltpu.SMEM], pltpu.VMEM
    plane = checkpoint[:, 0]
    tall = vmem((26, 72, DEPTH), f32)
    slots = call(pack_kernel, [(LINES, DEPTH)] * 6, [tall], 12, in_specs=smem + [on_chip])(place, plane)
    packed = dict(zip((0, 2, 3, 4, 5, 6), slots))

    plate = theta[after(tile_map, packed[0])]
    plate = jnp.broadcast_to(plate[:, :, None], (OWN, OWN, DEPTH))
    names = jnp.pad(tile_map.reshape(1, -1).astype(f32), ((0, 0), (0, DEPTH - OWN * OWN)))
    flags, names = lax.optimization_barrier((jnp.stack([solid_mask.astype(f32), plate]), names))
    packed[1], packed[7] = call(
        pack_flags_kernel, [(LINES + FLAG_LINES, DEPTH)] * 2, [tall], 12, in_specs=smem + [on_chip] * 2
    )(place, plane, flags)

    planes = [packed[0]] + [None] * 7
    for k in (5, 3, 1, 7, 2, 6, 4):
        planes[k] = neighbour(packed[k], "st", k)

    def both(value, axis):
        low, high = value
        low = neighbour(low, axis, 1)
        high = neighbour(high, axis, -1)
        return low, high

    halos = []
    lines = 2 * LINES + PLANE_FLAGS
    sent = call(route_first_kernel, [(lines, DEPTH)] * 2, (), 8, in_specs=smem + [on_chip] * 5)(
        place, planes[1], planes[5], planes[3], planes[7], flags
    )
    halos += both(sent, "gx")
    region, table = call(table_kernel, [(2, WIDE, WIDE, DEPTH), (WIDE, 20, WIDE, DEPTH)], mib=8)(
        planes[1], planes[7], flags, *halos
    )
    sent = call(route_second_kernel, [(2 * LINES, DEPTH)] * 2, (), 8, in_specs=smem + [on_chip] * 4)(
        place, planes[0], planes[4], planes[2], planes[6]
    )
    halos += both(sent, "gx")

    gl, gr = both((adjoint_in[:, 4:8], adjoint_in[:, 0:4]), "gx")
    tall = jnp.concatenate([gl, adjoint_in, gr], 1)
    slo, shi = both((tall[:, :, 4:8], tall[:, :, 0:4]), "st")

    big = (WIDE, 26, WIDE, DEPTH)
    mom, edge, edge_lo, edge_hi, heat = call(
        forward_kernel,
        [(3, WIDE, 4, WIDE, DEPTH), (OWN, 6, OWN, DEPTH), (OWN, 6, 4, DEPTH), (OWN, 6, 4, DEPTH), (1, DEPTH)],
        [vmem(big, f32), vmem(big, f32), vmem((WIDE, 4, WIDE, DEPTH), f32)],
        12,
        1,
        15,
    )(place, *planes, *halos, table, region)
    elo, ehi = both((edge_hi, edge_lo), "st")
    head, tail = call(merge_kernel, [(HALO, 6, WIDE, DEPTH)] * 2, mib=4)(elo, edge, ehi)
    el, er = both((tail, head), "gx")

    count = lax.axis_size("gx") * lax.axis_size("st")
    mine = (26, OWN, OWN, DEPTH)
    out_a, out_b, slots = call(
        backward_kernel,
        [mine, mine, (count, 2, DEPTH)],
        [vmem(big, f32)] * 4
        + [vmem((WIDE, 6, WIDE, DEPTH), f32), vmem((DEPTH, DEPTH), f32)]
        + [vmem(mine, f32)] * 2
        + [pltpu.SemaphoreType.DMA((2,))],
        24,
        out_specs=[pltpu.HBM, pltpu.HBM, pltpu.VMEM],
    )(adjoint_in, gl, gr, slo, shi, elo, edge, ehi, el, er, mom, table, region, names, heat)
    told = lax.all_to_all(slots, ("gx", "st"), 0, 0, tiled=True)

    scale = jnp.full((1,), 1.0 / (KAPPA * count * OWN * OWN), f32)
    tiles = (theta.shape[0] // DEPTH, DEPTH)
    theta_new, first_new, second_new, nusselt, adjoint = call(
        tile_kernel,
        [tiles] * 3 + [(1, 1), mine],
        [vmem(mine, f32)] * 2 + [pltpu.SemaphoreType.DMA((2,))],
        mib=12,
        in_specs=[pltpu.SMEM] + [pltpu.VMEM] * 4 + [pltpu.HBM] * 2,
        out_specs=[pltpu.VMEM] * 3 + [pltpu.SMEM, pltpu.VMEM],
    )(
        scale,
        told.reshape(2 * count, DEPTH),
        theta.reshape(tiles),
        first_moment.reshape(tiles),
        second_moment.reshape(tiles),
        out_a,
        out_b,
    )
    flat = theta.shape
    return (
        adjoint,
        theta_new.reshape(flat),
        first_new.reshape(flat),
        second_new.reshape(flat),
        nusselt.reshape(()),
    )


def solution(mesh):
    return jax.shard_map(
        window,
        mesh=mesh,
        in_specs=(
            P(None, ("gx", "st"), None, None),
            P(None, "gx", "st", None),
            P("gx", "st", None),
            P("gx", "st"),
            P(),
            P(),
            P(),
        ),
        out_specs=(P(None, "gx", "st", None), P(), P(), P(), P()),
        check_vma=False,
    )
```

profile of v0, /device:TPU:1, one launch (start us, length us, event | category | flops | bytes accessed | tf_op | source)
XLA Modules:
  0.0 124.6 jit_solution(12114820650856749112)
XLA Ops:
  0.7 1.1 copy-done.2
  1.8 1.9 %shard_map.110 = (f32[416,128]{1,0:T(8,128)S(1)}, f32[416,128]{1,0:T(8,128)S(1)}, f32[416,128]{1,0:T(8,128)}, f32[416,128]{1,0:T(8,128)S(1)}, f32[416,128]{1,0:T(8,128)S(1)}, /*index=5*/f32[416,128]{1,0:T(8,128)S(1)}) custom-call(s32[1]{0:T(128)} %bitcast.place, f32[26,64,128]{2,1,0:T(8,128)S(1)} %bitcast.13), custom_call_target="tpu_custom_call" | custom-call | tf_op jit(solution)/shard_map/pallas_call | solution.py:648
  3.7 4.3 %collective-permute-start.6 = (f32[416,128]{1,0:T(8,128)}, f32[416,128]{1,0:T(8,128)S(1)}, u32[]{:S(2)}, u32[]{:S(2)}) collective-permute-start(f32[416,128]{1,0:T(8,128)} %get-tuple-element.42), channel_id=1, source_target_pairs={{0,3},{1,4},{2,5},{3,6},{4,7},{5,0},{6,1},{7,2},{8,11},{9,12},{10,... | collective-permute-start | bytes 638984 | tf_op jit(solution)/shard_map/ppermute | solution.py:634
  8.0 2.1 %fusion.1 = (f32[26,4,8,128]{3,2,1,0:T(8,128)}, f32[26,4,8,128]{3,2,1,0:T(8,128)}) fusion(f32[26,8,8,128]{3,2,1,0:T(8,128)} %refs_0_.1), kind=kLoop, calls=%fused_computation.9 | loop fusion | bytes 1703936 | tf_op jit(solution)/shard_map/slice | solution.py:683
  10.1 1.2 collective-permute-start
  11.3 0.1 reshape.62
  11.4 0.8 gather_fusion
  12.2 0.1 reshape.61
  12.3 0.1 convert_element_type.21
  12.4 0.1 stack_broadcast_in_dim.2
  12.5 0.1 copy-done.3
  12.6 0.5 shard_map.111
  13.1 0.0 collective-permute-start.10
  13.1 1.7 %collective-permute-start.4 = (f32[480,128]{1,0:T(8,128)S(1)}, f32[480,128]{1,0:T(8,128)S(1)}, u32[]{:S(2)}, u32[]{:S(2)}) collective-permute-start(f32[480,128]{1,0:T(8,128)S(1)} %get-tuple-element.40), channel_id=1, source_target_pairs={{0,1},{1,2},{2,3},{3,4},{4,5},{5,6},{6,7},{7,0},{8,9},{9,10},{10,1... | collective-permute-start | bytes 737288 | tf_op jit(solution)/shard_map/ppermute | solution.py:634
  14.8 6.7 %collective-permute-start.1 = (f32[26,4,8,128]{3,2,1,0:T(8,128)}, f32[26,4,8,128]{3,2,1,0:T(8,128)S(1)}, u32[]{:S(2)}, u32[]{:S(2)}) collective-permute-start(f32[26,4,8,128]{3,2,1,0:T(8,128)} %get-tuple-element.71), channel_id=1, source_target_pairs={{0,248},{8,0},{16,8},{24,16},{32,24},{40,32},{48,40},{56,48},{64,5... | collective-permute-start | bytes 1277960 | tf_op jit(solution)/shard_map/ppermute | solution.py:634
  21.5 0.4 collective-permute-done.8.b.refs_5_
  21.9 1.6 %collective-permute-start.5 = (f32[416,128]{1,0:T(8,128)S(1)}, f32[416,128]{1,0:T(8,128)S(1)}, u32[]{:S(2)}, u32[]{:S(2)}) collective-permute-start(f32[416,128]{1,0:T(8,128)S(1)} %get-tuple-element.41), channel_id=1, source_target_pairs={{0,2},{1,3},{2,4},{3,5},{4,6},{5,7},{6,0},{7,1},{8,10},{9,11},{10,... | collective-permute-start | bytes 638984 | tf_op jit(solution)/shard_map/ppermute | solution.py:634
  23.5 3.6 %collective-permute-start.7 = (f32[416,128]{1,0:T(8,128)S(1)}, f32[416,128]{1,0:T(8,128)S(1)}, u32[]{:S(2)}, u32[]{:S(2)}) collective-permute-start(f32[416,128]{1,0:T(8,128)S(1)} %get-tuple-element.43), channel_id=1, source_target_pairs={{0,4},{1,5},{2,6},{3,7},{4,0},{5,1},{6,2},{7,3},{8,12},{9,13},{10,... | collective-permute-start | bytes 638984 | tf_op jit(solution)/shard_map/ppermute | solution.py:634
  27.1 0.2 shard_map.112
  27.3 1.0 collective-permute-start.11
  28.4 0.1 constant_dynamic-update-slice_fusion.1
  28.4 2.2 %collective-permute-done.1.refs_2_ = f32[26,4,8,128]{3,2,1,0:T(8,128)S(1)} collective-permute-done((f32[26,4,8,128]{3,2,1,0:T(8,128)}, f32[26,4,8,128]{3,2,1,0:T(8,128)S(1)}, u32[]{:S(2)}, u32[]{:S(2)}) %collective-permute-start.1) | collective-permute-done | bytes 426016 | tf_op jit(solution)/shard_map/ppermute | solution.py:634
  30.7 0.4 fusion
  31.2 1.7 %collective-permute-start.2 = (f32[26,16,4,128]{3,2,1,0:T(4,128)S(1)}, f32[26,16,4,128]{3,2,1,0:T(4,128)S(1)}, u32[]{:S(2)}, u32[]{:S(2)}) collective-permute-start(f32[26,16,4,128]{3,2,1,0:T(4,128)S(1)} %get-tuple-element.70), channel_id=1, source_target_pairs={{0,1},{1,2},{2,3},{3,4},{4,5},{5,6},{6,7},{7,0},{8,9},{9,10},{10,1... | collective-permute-start | bytes 2555912 | tf_op jit(solution)/shard_map/ppermute | solution.py:634
  32.9 4.0 %collective-permute-done.7.b.refs_4_ = f32[416,128]{1,0:T(8,128)S(1)} collective-permute-done((f32[416,128]{1,0:T(8,128)S(1)}, f32[416,128]{1,0:T(8,128)S(1)}, u32[]{:S(2)}, u32[]{:S(2)}) %collective-permute-start.7) | collective-permute-done | bytes 213024 | tf_op jit(solution)/shard_map/ppermute | solution.py:634
  36.9 5.1 %collective-permute-start.12 = (f32[960,128]{1,0:T(8,128)S(1)}, f32[960,128]{1,0:T(8,128)S(1)}, u32[]{:S(2)}, u32[]{:S(2)}) collective-permute-start(f32[960,128]{1,0:T(8,128)S(1)} %get-tuple-element.48), channel_id=1, source_target_pairs={{0,248},{8,0},{16,8},{24,16},{32,24},{40,32},{48,40},{56,48},{64,5... | collective-permute-start | bytes 1474568 | tf_op jit(solution)/shard_map/ppermute | solution.py:634
  42.0 0.2 shard_map.113
  42.2 0.1 collective-permute-start.13
  42.3 3.1 %collective-permute-done.11.from_left.refs_8_ = f32[960,128]{1,0:T(8,128)S(1)} collective-permute-done((f32[960,128]{1,0:T(8,128)S(1)}, f32[960,128]{1,0:T(8,128)S(1)}, u32[]{:S(2)}, u32[]{:S(2)}) %collective-permute-start.11) | collective-permute-done | bytes 491552 | tf_op jit(solution)/shard_map/ppermute | solution.py:634
  45.4 1.6 %collective-permute-start.14 = (f32[832,128]{1,0:T(8,128)S(1)}, f32[832,128]{1,0:T(8,128)S(1)}, u32[]{:S(2)}, u32[]{:S(2)}) collective-permute-start(f32[832,128]{1,0:T(8,128)S(1)} %get-tuple-element.50), channel_id=1, source_target_pairs={{0,248},{8,0},{16,8},{24,16},{32,24},{40,32},{48,40},{56,48},{64,5... | collective-permute-start | bytes 1277960 | tf_op jit(solution)/shard_map/ppermute | solution.py:634
  47.0 6.0 %collective-permute-done.12.from_right.refs_9_ = f32[960,128]{1,0:T(8,128)S(1)} collective-permute-done((f32[960,128]{1,0:T(8,128)S(1)}, f32[960,128]{1,0:T(8,128)S(1)}, u32[]{:S(2)}, u32[]{:S(2)}) %collective-permute-start.12) | collective-permute-done | bytes 491552 | tf_op jit(solution)/shard_map/ppermute | solution.py:634
  53.0 1.3 %shard_map.114 = (f32[2,16,16,128]{3,2,1,0:T(8,128)S(1)}, f32[16,20,16,128]{3,2,1,0:T(8,128)S(1)}) custom-call(f32[480,128]{1,0:T(8,128)S(1)} %collective-permute-done.4.a.low.refs_1_, f32[480,128]{1,0:T(8,128)S(1)} %collective-permute-done.10.d.high.refs_7_, f32[2,8,8,128]{3,2,1,0:T(8,128)S(1)} %pad_maximum_fusion.flags, ...), custom_call_target="tpu_custom_call" | custom-call | tf_op jit(solution)/shard_map/pallas_call | solution.py:675
  54.3 2.4 %collective-permute-done.13.refs_10_ = f32[832,128]{1,0:T(8,128)S(1)} collective-permute-done((f32[832,128]{1,0:T(8,128)S(1)}, f32[832,128]{1,0:T(8,128)S(1)}, u32[]{:S(2)}, u32[]{:S(2)}) %collective-permute-start.13) | collective-permute-done | bytes 426016 | tf_op jit(solution)/shard_map/ppermute | solution.py:634
  56.7 4.8 %collective-permute-done.14.refs_11_ = f32[832,128]{1,0:T(8,128)S(1)} collective-permute-done((f32[832,128]{1,0:T(8,128)S(1)}, f32[832,128]{1,0:T(8,128)S(1)}, u32[]{:S(2)}, u32[]{:S(2)}) %collective-permute-start.14) | collective-permute-done | bytes 426016 | tf_op jit(solution)/shard_map/ppermute | solution.py:634
  61.5 6.7 %shard_map.115 = (f32[3,16,4,16,128]{4,3,2,1,0:T(8,128)S(1)}, f32[8,6,8,128]{3,2,1,0:T(8,128)S(1)}, f32[8,6,4,128]{3,2,1,0:T(4,128)S(1)}, f32[8,6,4,128]{3,2,1,0:T(4,128)S(1)}, f32[1,128]{1,0:T(1,128)S(1)}) custom-call(s32[1]{0:T(128)} %bitcast.place, f32[416,128]{1,0:T(8,128)S(1)} %get-tuple-element.37.a.refs_0_, ...), custom_call_target="tpu_custom_call" | custom-call | tf_op jit(solution)/shard_map/pallas_call | solution.py:688
  68.2 0.0 collective-permute-start.15
  68.2 0.5 collective-permute-start.16
  68.7 1.1 collective-permute-done.15.lo.refs_5_
  69.8 2.7 %collective-permute-done.16.hi.refs_7_ = f32[8,6,4,128]{3,2,1,0:T(4,128)S(1)} collective-permute-done((f32[8,6,4,128]{3,2,1,0:T(4,128)S(1)}, f32[8,6,4,128]{3,2,1,0:T(4,128)S(1)}, u32[]{:S(2)}, u32[]{:S(2)}) %collective-permute-start.16) | collective-permute-done | bytes 98336 | tf_op jit(solution)/shard_map/ppermute | solution.py:634
  72.5 0.1 shard_map.116
  72.6 0.1 collective-permute-start.17
  72.7 5.5 %collective-permute-start.18 = (f32[4,6,16,128]{3,2,1,0:T(8,128)S(1)}, f32[4,6,16,128]{3,2,1,0:T(8,128)S(1)}, u32[]{:S(2)}, u32[]{:S(2)}) collective-permute-start(f32[4,6,16,128]{3,2,1,0:T(8,128)S(1)} %get-tuple-element.57), channel_id=1, source_target_pairs={{0,248},{8,0},{16,8},{24,16},{32,24},{40,32},{48,40},{56,48},{64,5... | collective-permute-start | bytes 589832 | tf_op jit(solution)/shard_map/ppermute | solution.py:634
  78.2 4.1 %collective-permute-done.17.refs_8_ = f32[4,6,16,128]{3,2,1,0:T(8,128)S(1)} collective-permute-done((f32[4,6,16,128]{3,2,1,0:T(8,128)S(1)}, f32[4,6,16,128]{3,2,1,0:T(8,128)S(1)}, u32[]{:S(2)}, u32[]{:S(2)}) %collective-permute-start.17) | collective-permute-done | bytes 196640 | tf_op jit(solution)/shard_map/ppermute | solution.py:634
  82.3 0.0 copy-start.4
  82.3 0.0 copy-start.5
  82.3 11.0 %shard_map.117 = (f32[26,8,8,128]{3,2,1,0:T(8,128)S(1)}, f32[26,8,8,128]{3,2,1,0:T(8,128)S(1)}, f32[256,2,128]{2,1,0:T(2,128)S(1)}) custom-call(f32[26,8,8,128]{3,2,1,0:T(8,128)S(1)} %copy-done.1, f32[26,4,8,128]{3,2,1,0:T(8,128)S(1)} %collective-permute-done.refs_1_, f32[26,4,8,128]{3,2,1,0:T(8,128)S(1)} %collective-permute-done.1.refs_2_, ...), custom_call_target="tpu_custom_call" | custom-call | tf_op jit(solution)/shard_map/pallas_call | solution.py:702
  93.3 26.1 %all_to_all.5 = f32[256,2,128]{2,1,0:T(2,128)S(1)} all-to-all(f32[256,2,128]{2,1,0:T(2,128)S(1)} %get-tuple-element.61), channel_id=1, replica_groups=mesh['gx'=32,'st'=8] {'gx','st'}, dimensions={0} | all-to-all | bytes 524288 | tf_op jit(solution)/shard_map/all_to_all | solution.py:712
  119.5 5.0 %shard_map.118 = (f32[32,128]{1,0:T(8,128)}, f32[32,128]{1,0:T(8,128)}, f32[32,128]{1,0:T(8,128)}, f32[1,1]{1,0:T(1,128)}, f32[26,8,8,128]{3,2,1,0:T(8,128)}) custom-call(f32[1]{0:T(128)} %constant.5.clone.1.scale, f32[512,128]{1,0:T(8,128)S(1)} %bitcast.15, f32[32,128]{1,0:T(8,128)S(1)} %bitcast.12, f32[32,128]{1,0:T(8,128)S(1)} %bitcast.16, ...), custom_call_target="tpu_custom_call" | custom-call | tf_op jit(solution)/shard_map/pallas_call | solution.py:716
  (32 shorter events, 0.1 us)
Async XLA Ops:
  0.6 10.8 %copy-start = (f32[4096]{0:T(1024)S(1)}, f32[4096]{0:T(1024)}, u32[]{:S(2)}) copy-start(f32[4096]{0:T(1024)} %param.11) | copy-start | bytes 49156
  0.6 1.2 copy-start.2
  1.8 9.5 %copy-start.7 = (s32[8,8]{1,0:T(8,128)S(1)}, s32[8,8]{1,0:T(8,128)}, u32[]{:S(2)}) copy-start(s32[8,8]{1,0:T(8,128)} %param.10) | copy-start | bytes 772
  1.8 9.6 %copy-start.6 = (s32[8,8,128]{2,1,0:T(8,128)S(1)}, s32[8,8,128]{2,1,0:T(8,128)}, u32[]{:S(2)}) copy-start(s32[8,8,128]{2,1,0:T(8,128)} %param.9) | copy-start | bytes 98308
  3.7 11.2 %collective-permute-start.6 = (f32[416,128]{1,0:T(8,128)}, f32[416,128]{1,0:T(8,128)S(1)}, u32[]{:S(2)}, u32[]{:S(2)}) collective-permute-start(f32[416,128]{1,0:T(8,128)} %get-tuple-element.42), channel_id=1, source_target_pairs={{0,3},{1,4},{2,5},{3,6},{4,7},{5,0},{6,1},{7,2},{8,11},{9,12},{10,... | collective-permute-start | bytes 638984 | tf_op jit(solution)/shard_map/ppermute | solution.py:634
  10.1 17.3 %collective-permute-start = (f32[26,4,8,128]{3,2,1,0:T(8,128)}, f32[26,4,8,128]{3,2,1,0:T(8,128)S(1)}, u32[]{:S(2)}, u32[]{:S(2)}) collective-permute-start(f32[26,4,8,128]{3,2,1,0:T(8,128)} %get-tuple-element.72), channel_id=1, source_target_pairs={{0,8},{8,16},{16,24},{24,32},{32,40},{40,48},{48,56},{56,64},{64,7... | collective-permute-start | bytes 1277960 | tf_op jit(solution)/shard_map/ppermute | solution.py:634
  11.4 1.2 copy-start.3
  12.2 16.2 %copy-start.1 = (f32[26,8,8,128]{3,2,1,0:T(8,128)S(1)}, f32[26,8,8,128]{3,2,1,0:T(8,128)}, u32[]{:S(2)}) copy-start(f32[26,8,8,128]{3,2,1,0:T(8,128)} %refs_0_.1) | copy-start | bytes 2555908
  13.1 10.5 %collective-permute-start.10 = (f32[480,128]{1,0:T(8,128)S(1)}, f32[480,128]{1,0:T(8,128)S(1)}, u32[]{:S(2)}, u32[]{:S(2)}) collective-permute-start(f32[480,128]{1,0:T(8,128)S(1)} %get-tuple-element.46), channel_id=1, source_target_pairs={{0,7},{1,0},{2,1},{3,2},{4,3},{5,4},{6,5},{7,6},{8,15},{9,8},{10,9... | collective-permute-start | bytes 737288 | tf_op jit(solution)/shard_map/ppermute | solution.py:634
  13.1 14.1 %collective-permute-start.4 = (f32[480,128]{1,0:T(8,128)S(1)}, f32[480,128]{1,0:T(8,128)S(1)}, u32[]{:S(2)}, u32[]{:S(2)}) collective-permute-start(f32[480,128]{1,0:T(8,128)S(1)} %get-tuple-element.40), channel_id=1, source_target_pairs={{0,1},{1,2},{2,3},{3,4},{4,5},{5,6},{6,7},{7,0},{8,9},{9,10},{10,1... | collective-permute-start | bytes 737288 | tf_op jit(solution)/shard_map/ppermute | solution.py:634
  14.8 7.1 %collective-permute-start.8 = (f32[416,128]{1,0:T(8,128)S(1)}, f32[416,128]{1,0:T(8,128)S(1)}, u32[]{:S(2)}, u32[]{:S(2)}) collective-permute-start(f32[416,128]{1,0:T(8,128)S(1)} %get-tuple-element.44), channel_id=1, source_target_pairs={{0,5},{1,6},{2,7},{3,0},{4,1},{5,2},{6,3},{7,4},{8,13},{9,14},{10,... | collective-permute-start | bytes 638984 | tf_op jit(solution)/shard_map/ppermute | solution.py:634
  14.8 15.9 %collective-permute-start.1 = (f32[26,4,8,128]{3,2,1,0:T(8,128)}, f32[26,4,8,128]{3,2,1,0:T(8,128)S(1)}, u32[]{:S(2)}, u32[]{:S(2)}) collective-permute-start(f32[26,4,8,128]{3,2,1,0:T(8,128)} %get-tuple-element.71), channel_id=1, source_target_pairs={{0,248},{8,0},{16,8},{24,16},{32,24},{40,32},{48,40},{56,48},{64,5... | collective-permute-start | bytes 1277960 | tf_op jit(solution)/shard_map/ppermute | solution.py:634
  21.9 11.0 %collective-permute-start.5 = (f32[416,128]{1,0:T(8,128)S(1)}, f32[416,128]{1,0:T(8,128)S(1)}, u32[]{:S(2)}, u32[]{:S(2)}) collective-permute-start(f32[416,128]{1,0:T(8,128)S(1)} %get-tuple-element.41), channel_id=1, source_target_pairs={{0,2},{1,3},{2,4},{3,5},{4,6},{5,7},{6,0},{7,1},{8,10},{9,11},{10,... | collective-permute-start | bytes 638984 | tf_op jit(solution)/shard_map/ppermute | solution.py:634
  23.5 13.3 %collective-permute-start.7 = (f32[416,128]{1,0:T(8,128)S(1)}, f32[416,128]{1,0:T(8,128)S(1)}, u32[]{:S(2)}, u32[]{:S(2)}) collective-permute-start(f32[416,128]{1,0:T(8,128)S(1)} %get-tuple-element.43), channel_id=1, source_target_pairs={{0,4},{1,5},{2,6},{3,7},{4,0},{5,1},{6,2},{7,3},{8,12},{9,13},{10,... | collective-permute-start | bytes 638984 | tf_op jit(solution)/shard_map/ppermute | solution.py:634
  27.1 14.9 %collective-permute-start.9 = (f32[416,128]{1,0:T(8,128)S(1)}, f32[416,128]{1,0:T(8,128)S(1)}, u32[]{:S(2)}, u32[]{:S(2)}) collective-permute-start(f32[416,128]{1,0:T(8,128)S(1)} %get-tuple-element.45), channel_id=1, source_target_pairs={{0,6},{1,7},{2,0},{3,1},{4,2},{5,3},{6,4},{7,5},{8,14},{9,15},{10,... | collective-permute-start | bytes 638984 | tf_op jit(solution)/shard_map/ppermute | solution.py:634
  27.3 18.1 %collective-permute-start.11 = (f32[960,128]{1,0:T(8,128)S(1)}, f32[960,128]{1,0:T(8,128)S(1)}, u32[]{:S(2)}, u32[]{:S(2)}) collective-permute-start(f32[960,128]{1,0:T(8,128)S(1)} %get-tuple-element.47), channel_id=1, source_target_pairs={{0,8},{8,16},{16,24},{24,32},{32,40},{40,48},{48,56},{56,64},{64,7... | collective-permute-start | bytes 1474568 | tf_op jit(solution)/shard_map/ppermute | solution.py:634
  31.2 51.1 %collective-permute-start.2 = (f32[26,16,4,128]{3,2,1,0:T(4,128)S(1)}, f32[26,16,4,128]{3,2,1,0:T(4,128)S(1)}, u32[]{:S(2)}, u32[]{:S(2)}) collective-permute-start(f32[26,16,4,128]{3,2,1,0:T(4,128)S(1)} %get-tuple-element.70), channel_id=1, source_target_pairs={{0,1},{1,2},{2,3},{3,4},{4,5},{5,6},{6,7},{7,0},{8,9},{9,10},{10,1... | collective-permute-start | bytes 2555912 | tf_op jit(solution)/shard_map/ppermute | solution.py:634
  32.9 49.4 %collective-permute-start.3 = (f32[26,16,4,128]{3,2,1,0:T(4,128)S(1)}, f32[26,16,4,128]{3,2,1,0:T(4,128)S(1)}, u32[]{:S(2)}, u32[]{:S(2)}) collective-permute-start(f32[26,16,4,128]{3,2,1,0:T(4,128)S(1)} %get-tuple-element.69), channel_id=1, source_target_pairs={{0,7},{1,0},{2,1},{3,2},{4,3},{5,4},{6,5},{7,6},{8,15},{9,8},{10,9... | collective-permute-start | bytes 2555912 | tf_op jit(solution)/shard_map/ppermute | solution.py:634
  36.9 16.2 %collective-permute-start.12 = (f32[960,128]{1,0:T(8,128)S(1)}, f32[960,128]{1,0:T(8,128)S(1)}, u32[]{:S(2)}, u32[]{:S(2)}) collective-permute-start(f32[960,128]{1,0:T(8,128)S(1)} %get-tuple-element.48), channel_id=1, source_target_pairs={{0,248},{8,0},{16,8},{24,16},{32,24},{40,32},{48,40},{56,48},{64,5... | collective-permute-start | bytes 1474568 | tf_op jit(solution)/shard_map/ppermute | solution.py:634
  42.2 14.5 %collective-permute-start.13 = (f32[832,128]{1,0:T(8,128)S(1)}, f32[832,128]{1,0:T(8,128)S(1)}, u32[]{:S(2)}, u32[]{:S(2)}) collective-permute-start(f32[832,128]{1,0:T(8,128)S(1)} %get-tuple-element.49), channel_id=1, source_target_pairs={{0,8},{8,16},{16,24},{24,32},{32,40},{40,48},{48,56},{56,64},{64,7... | collective-permute-start | bytes 1277960 | tf_op jit(solution)/shard_map/ppermute | solution.py:634
  45.4 16.0 %collective-permute-start.14 = (f32[832,128]{1,0:T(8,128)S(1)}, f32[832,128]{1,0:T(8,128)S(1)}, u32[]{:S(2)}, u32[]{:S(2)}) collective-permute-start(f32[832,128]{1,0:T(8,128)S(1)} %get-tuple-element.50), channel_id=1, source_target_pairs={{0,248},{8,0},{16,8},{24,16},{32,24},{40,32},{48,40},{56,48},{64,5... | collective-permute-start | bytes 1277960 | tf_op jit(solution)/shard_map/ppermute | solution.py:634
  68.2 1.7 %collective-permute-start.15 = (f32[8,6,4,128]{3,2,1,0:T(4,128)S(1)}, f32[8,6,4,128]{3,2,1,0:T(4,128)S(1)}, u32[]{:S(2)}, u32[]{:S(2)}) collective-permute-start(f32[8,6,4,128]{3,2,1,0:T(4,128)S(1)} %get-tuple-element.53), channel_id=1, source_target_pairs={{0,1},{1,2},{2,3},{3,4},{4,5},{5,6},{6,7},{7,0},{8,9},{9,10},{10,1... | collective-permute-start | bytes 294920 | tf_op jit(solution)/shard_map/ppermute | solution.py:634
  68.2 4.3 %collective-permute-start.16 = (f32[8,6,4,128]{3,2,1,0:T(4,128)S(1)}, f32[8,6,4,128]{3,2,1,0:T(4,128)S(1)}, u32[]{:S(2)}, u32[]{:S(2)}) collective-permute-start(f32[8,6,4,128]{3,2,1,0:T(4,128)S(1)} %get-tuple-element.55), channel_id=1, source_target_pairs={{0,7},{1,0},{2,1},{3,2},{4,3},{5,4},{6,5},{7,6},{8,15},{9,8},{10,9... | collective-permute-start | bytes 294920 | tf_op jit(solution)/shard_map/ppermute | solution.py:634
  72.6 9.7 %collective-permute-start.17 = (f32[4,6,16,128]{3,2,1,0:T(8,128)S(1)}, f32[4,6,16,128]{3,2,1,0:T(8,128)S(1)}, u32[]{:S(2)}, u32[]{:S(2)}) collective-permute-start(f32[4,6,16,128]{3,2,1,0:T(8,128)S(1)} %get-tuple-element.56), channel_id=1, source_target_pairs={{0,8},{8,16},{16,24},{24,32},{32,40},{40,48},{48,56},{56,64},{64,7... | collective-permute-start | bytes 589832 | tf_op jit(solution)/shard_map/ppermute | solution.py:634
  72.7 9.6 %collective-permute-start.18 = (f32[4,6,16,128]{3,2,1,0:T(8,128)S(1)}, f32[4,6,16,128]{3,2,1,0:T(8,128)S(1)}, u32[]{:S(2)}, u32[]{:S(2)}) collective-permute-start(f32[4,6,16,128]{3,2,1,0:T(8,128)S(1)} %get-tuple-element.57), channel_id=1, source_target_pairs={{0,248},{8,0},{16,8},{24,16},{32,24},{40,32},{48,40},{56,48},{64,5... | collective-permute-start | bytes 589832 | tf_op jit(solution)/shard_map/ppermute | solution.py:634
  82.3 37.1 %copy-start.4 = (f32[4096]{0:T(1024)S(1)}, f32[4096]{0:T(1024)}, u32[]{:S(2)}) copy-start(f32[4096]{0:T(1024)} %param.12) | copy-start | bytes 49156
  82.3 37.1 %copy-start.5 = (f32[4096]{0:T(1024)S(1)}, f32[4096]{0:T(1024)}, u32[]{:S(2)}) copy-start(f32[4096]{0:T(1024)} %param.13) | copy-start | bytes 49156
where the time goes:
time: 125 us
  starting transfers between devices  34.8 us (28%)
  waiting for transfers between devices  30.9 us (25%)
  Pallas kernels  26.6 us (21%)
  blocking collectives  26.1 us (21%)
  local copies, waits for them, and re-layouts  5.05 us (4%)
    ppermute x19, starting transfers between devices, neighbour(): lax.ppermute(value, axis, [(i, (i + step) % count) for i in range(count)])  34.8 us
    ppermute x19, waiting for transfers between devices, neighbour(): lax.ppermute(value, axis, [(i, (i + step) % count) for i in range(count)])  30.9 us
    all_to_all x1, blocking collectives, window(): told = lax.all_to_all(slots, ('gx', 'st'), 0, 0, tiled=True)  26.1 us
    pallas_call x1, Pallas kernels, window(): call(backward_kernel, [mine, mine, (count, 2, DEPTH)], [vmem(big, f32)] *...  11 us
    pallas_call x1, Pallas kernels, window(): call(forward_kernel, [(3, WIDE, 4, WIDE, DEPTH), (OWN, 6, OWN, DEPTH), (O...  6.7 us
    pallas_call x1, Pallas kernels, window(): call(tile_kernel, [tiles] * 3 + [(1, 1), mine], [vmem(mine, f32)] * 2 + [...  4.98 us
  transfers between devices with their start and end apart: 19, of which 10 were waited for; matrix products, arithmetic and copies ran while one was open for 3% of the time, Pallas kernels for 7%

commit v1 on v0

--- a/solution.py
+++ b/solution.py
@@ -461,18 +461,20 @@
     own, gl, gr, slo, shi, elo, emid, ehi, el, er, mom, table, region, names, heat = refs[:15]
     out_a, out_b, slots, la0, la1, lb0, lb1, late, sums, last_a, last_b, sems = refs[15:]
 
-    def gather(src, count, off):
-        def one(x):
-            for i in range(26):
-                la0[x + off, i, 0:4] = slo[i, x + off]
-                la0[x + off, i, 4:12] = src[i, x]
-                la0[x + off, i, 12:16] = shi[i, x + off]
-
-        loop(count, one)
-
-    gather(gl, HALO, 0)
-    gather(own, OWN, HALO)
-    gather(gr, HALO, HALO + OWN)
+    def gather(x):
+        for i in range(26):
+            la0[x + HALO, i, 0:4] = slo[i, x]
+            la0[x + HALO, i, 4:12] = own[i, x]
+            la0[x + HALO, i, 12:16] = shi[i, x]
+
+    loop(OWN, gather)
+
+    def beside(x):
+        for i in range(26):
+            la0[x, i] = gl[i, x]
+            la0[x + HALO + OWN, i] = gr[i, x]
+
+    loop(HALO, beside)
 
     def settle(x):
         for a in range(6):
@@ -680,9 +682,13 @@
     )
     halos += both(sent, "gx")
 
-    gl, gr = both((adjoint_in[:, 4:8], adjoint_in[:, 0:4]), "gx")
-    tall = jnp.concatenate([gl, adjoint_in, gr], 1)
-    slo, shi = both((tall[:, :, 4:8], tall[:, :, 0:4]), "st")
+    slo, shi = both((adjoint_in[:, :, 4:8], adjoint_in[:, :, 0:4]), "st")
+
+    def rows(first):
+        part = slice(first, first + HALO)
+        return jnp.concatenate([slo[:, part], adjoint_in[:, part], shi[:, part]], 2)
+
+    gl, gr = both((rows(HALO), rows(0)), "gx")
 
     big = (WIDE, 26, WIDE, DEPTH)
     mom, edge, edge_lo, edge_hi, heat = call(

time: 125 us -> 138 us (1.10)
  waiting for transfers between devices: 30.9 us -> 42.7 us
  blocking collectives: 26.1 us -> 24.1 us
  starting transfers between devices: 34.8 us -> 36.8 us
  other arithmetic: 0.02 us -> 1.89 us
    ppermute x19, waiting for transfers between devices: 30.9 us -> 42.7 us  [neighbour(): lax.ppermute(value, axis, [(i, (i + step) % count) for i in range(count)])]
    all_to_all x1, blocking collectives: 26.1 us -> 24.1 us  [window(): told = lax.all_to_all(slots, ('gx', 'st'), 0, 0, tiled=True)]
    ppermute x19, starting transfers between devices: 34.8 us -> 36.8 us  [neighbour(): lax.ppermute(value, axis, [(i, (i + step) % count) for i in range(count)])]
  transfers between devices with their start and end apart: 19 -> 19, of which waited for: 10 -> 8; matrix products, arithmetic and copies ran while one was open for 3% -> 4% of each run, Pallas kernels for 7% -> 6%
where the time goes in v1:
time: 138 us
  waiting for transfers between devices  42.7 us (31%)
  starting transfers between devices  36.8 us (27%)
  Pallas kernels  26.5 us (19%)
  blocking collectives  24.1 us (17%)
  local copies, waits for them, and re-layouts  4.89 us (4%)
  other arithmetic  1.89 us (1%)
    ppermute x19, waiting for transfers between devices, neighbour(): lax.ppermute(value, axis, [(i, (i + step) % count) for i in range(count)])  42.7 us
    ppermute x19, starting transfers between devices, neighbour(): lax.ppermute(value, axis, [(i, (i + step) % count) for i in range(count)])  36.8 us
    all_to_all x1, blocking collectives, window(): told = lax.all_to_all(slots, ('gx', 'st'), 0, 0, tiled=True)  24.1 us
    pallas_call x1, Pallas kernels, window(): call(backward_kernel, [mine, mine, (count, 2, DEPTH)], [vmem(big, f32)] *...  10.8 us
    pallas_call x1, Pallas kernels, window(): call(forward_kernel, [(3, WIDE, 4, WIDE, DEPTH), (OWN, 6, OWN, DEPTH), (O...  6.69 us
    pallas_call x1, Pallas kernels, window(): call(tile_kernel, [tiles] * 3 + [(1, 1), mine], [vmem(mine, f32)] * 2 + [...  4.98 us
  transfers between devices with their start and end apart: 19, of which 8 were waited for; matrix products, arithmetic and copies ran while one was open for 4% of the time, Pallas kernels for 6%

profile of v1, /device:TPU:1, one launch (start us, length us, event | category | flops | bytes accessed | tf_op | source)
XLA Modules:
  0.0 138.0 jit_solution(15218117079801167730)
XLA Ops:
  0.6 0.0 copy-start.2
  0.7 1.1 copy-done.2
  1.8 1.8 %shard_map.110 = (f32[416,128]{1,0:T(8,128)S(1)}, f32[416,128]{1,0:T(8,128)S(1)}, f32[416,128]{1,0:T(8,128)}, f32[416,128]{1,0:T(8,128)S(1)}, f32[416,128]{1,0:T(8,128)S(1)}, /*index=5*/f32[416,128]{1,0:T(8,128)S(1)}) custom-call(s32[1]{0:T(128)} %bitcast.place, f32[26,64,128]{2,1,0:T(8,128)S(1)} %bitcast.13), custom_call_target="tpu_custom_call" | custom-call | tf_op jit(solution)/shard_map/pallas_call | solution.py:650
  3.6 4.3 %collective-permute-start.6 = (f32[416,128]{1,0:T(8,128)}, f32[416,128]{1,0:T(8,128)S(1)}, u32[]{:S(2)}, u32[]{:S(2)}) collective-permute-start(f32[416,128]{1,0:T(8,128)} %get-tuple-element.42), channel_id=1, source_target_pairs={{0,3},{1,4},{2,5},{3,6},{4,7},{5,0},{6,1},{7,2},{8,11},{9,12},{10,... | collective-permute-start | bytes 638984 | tf_op jit(solution)/shard_map/ppermute | solution.py:636
  7.9 2.5 %fusion.1 = (f32[26,8,4,128]{3,2,1,0:T(4,128)}, f32[26,8,4,128]{3,2,1,0:T(4,128)}) fusion(f32[26,8,8,128]{3,2,1,0:T(8,128)} %refs_0_.1), kind=kLoop, calls=%fused_computation.8 | loop fusion | bytes 1703936 | tf_op jit(solution)/shard_map/slice | solution.py:685
  10.4 0.8 compare_select_fusion
  11.2 0.1 reshape.62
  11.3 0.8 convert_bitcast_fusion
  12.1 0.0 copy-start.1
  12.1 0.8 gather_fusion
  12.9 0.1 reshape.61
  13.0 0.1 convert_element_type.21
  13.1 0.1 stack_broadcast_in_dim.2
  13.1 0.5 shard_map.111
  13.7 0.4 collective-permute-start.10
  14.1 1.3 collective-permute-start.4
  15.4 0.6 collective-permute-start.8
  16.0 1.6 %collective-permute-start.1 = (f32[26,8,4,128]{3,2,1,0:T(4,128)}, f32[26,8,4,128]{3,2,1,0:T(4,128)S(1)}, u32[]{:S(2)}, u32[]{:S(2)}) collective-permute-start(f32[26,8,4,128]{3,2,1,0:T(4,128)} %get-tuple-element.72), channel_id=1, source_target_pairs={{0,7},{1,0},{2,1},{3,2},{4,3},{5,4},{6,5},{7,6},{8,15},{9,8},{10,9... | collective-permute-start | bytes 1277960 | tf_op jit(solution)/shard_map/ppermute | solution.py:636
  17.6 0.1 fusion
  17.6 6.5 %collective-permute-done.8.b.refs_5_ = f32[416,128]{1,0:T(8,128)S(1)} collective-permute-done((f32[416,128]{1,0:T(8,128)S(1)}, f32[416,128]{1,0:T(8,128)S(1)}, u32[]{:S(2)}, u32[]{:S(2)}) %collective-permute-start.8) | collective-permute-done | bytes 213024 | tf_op jit(solution)/shard_map/ppermute | solution.py:636
  24.2 1.0 collective-permute-start.5
  25.1 2.4 %collective-permute-start.7 = (f32[416,128]{1,0:T(8,128)S(1)}, f32[416,128]{1,0:T(8,128)S(1)}, u32[]{:S(2)}, u32[]{:S(2)}) collective-permute-start(f32[416,128]{1,0:T(8,128)S(1)} %get-tuple-element.43), channel_id=1, source_target_pairs={{0,4},{1,5},{2,6},{3,7},{4,0},{5,1},{6,2},{7,3},{8,12},{9,13},{10,... | collective-permute-start | bytes 638984 | tf_op jit(solution)/shard_map/ppermute | solution.py:636
  27.5 0.2 shard_map.112
  27.7 1.3 collective-permute-start.11
  29.1 0.2 pad_maximum_fusion.1
  29.3 8.1 %collective-permute-start.3 = (f32[26,4,16,128]{3,2,1,0:T(8,128)S(1)}, f32[26,4,16,128]{3,2,1,0:T(8,128)S(1)}, u32[]{:S(2)}, u32[]{:S(2)}) collective-permute-start(f32[26,4,16,128]{3,2,1,0:T(8,128)S(1)} %pad_maximum_fusion.1), channel_id=1, source_target_pairs={{0,248},{8,0},{16,8},{24,16},{32,24},{40,32},{48,40},{56,48},{64,5... | collective-permute-start | bytes 2555912 | tf_op jit(solution)/shard_map/ppermute | solution.py:636
  37.4 0.2 pad_maximum_fusion
  37.6 0.1 collective-permute-start.2
  37.7 6.4 %collective-permute-start.12 = (f32[960,128]{1,0:T(8,128)S(1)}, f32[960,128]{1,0:T(8,128)S(1)}, u32[]{:S(2)}, u32[]{:S(2)}) collective-permute-start(f32[960,128]{1,0:T(8,128)S(1)} %get-tuple-element.48), channel_id=1, source_target_pairs={{0,248},{8,0},{16,8},{24,16},{32,24},{40,32},{48,40},{56,48},{64,5... | collective-permute-start | bytes 1474568 | tf_op jit(solution)/shard_map/ppermute | solution.py:636
  44.1 0.2 shard_map.113
  44.3 0.1 collective-permute-start.13
  44.3 2.1 %collective-permute-done.11.from_left.refs_8_ = f32[960,128]{1,0:T(8,128)S(1)} collective-permute-done((f32[960,128]{1,0:T(8,128)S(1)}, f32[960,128]{1,0:T(8,128)S(1)}, u32[]{:S(2)}, u32[]{:S(2)}) %collective-permute-start.11) | collective-permute-done | bytes 491552 | tf_op jit(solution)/shard_map/ppermute | solution.py:636
  46.4 2.7 %collective-permute-start.14 = (f32[832,128]{1,0:T(8,128)S(1)}, f32[832,128]{1,0:T(8,128)S(1)}, u32[]{:S(2)}, u32[]{:S(2)}) collective-permute-start(f32[832,128]{1,0:T(8,128)S(1)} %get-tuple-element.50), channel_id=1, source_target_pairs={{0,248},{8,0},{16,8},{24,16},{32,24},{40,32},{48,40},{56,48},{64,5... | collective-permute-start | bytes 1277960 | tf_op jit(solution)/shard_map/ppermute | solution.py:636
  49.1 17.6 %collective-permute-done.12.from_right.refs_9_ = f32[960,128]{1,0:T(8,128)S(1)} collective-permute-done((f32[960,128]{1,0:T(8,128)S(1)}, f32[960,128]{1,0:T(8,128)S(1)}, u32[]{:S(2)}, u32[]{:S(2)}) %collective-permute-start.12) | collective-permute-done | bytes 491552 | tf_op jit(solution)/shard_map/ppermute | solution.py:636
  66.7 1.3 shard_map.114
  68.0 5.8 %collective-permute-done.13.refs_10_ = f32[832,128]{1,0:T(8,128)S(1)} collective-permute-done((f32[832,128]{1,0:T(8,128)S(1)}, f32[832,128]{1,0:T(8,128)S(1)}, u32[]{:S(2)}, u32[]{:S(2)}) %collective-permute-start.13) | collective-permute-done | bytes 426016 | tf_op jit(solution)/shard_map/ppermute | solution.py:636
  73.8 1.8 %collective-permute-done.14.refs_11_ = f32[832,128]{1,0:T(8,128)S(1)} collective-permute-done((f32[832,128]{1,0:T(8,128)S(1)}, f32[832,128]{1,0:T(8,128)S(1)}, u32[]{:S(2)}, u32[]{:S(2)}) %collective-permute-start.14) | collective-permute-done | bytes 426016 | tf_op jit(solution)/shard_map/ppermute | solution.py:636
  75.6 6.7 %shard_map.115 = (f32[3,16,4,16,128]{4,3,2,1,0:T(8,128)S(1)}, f32[8,6,8,128]{3,2,1,0:T(8,128)S(1)}, f32[8,6,4,128]{3,2,1,0:T(4,128)S(1)}, f32[8,6,4,128]{3,2,1,0:T(4,128)S(1)}, f32[1,128]{1,0:T(1,128)S(1)}) custom-call(s32[1]{0:T(128)} %bitcast.place, f32[416,128]{1,0:T(8,128)S(1)} %get-tuple-element.37.a.refs_0_, ...), custom_call_target="tpu_custom_call" | custom-call | tf_op jit(solution)/shard_map/pallas_call | solution.py:694
  82.3 0.7 collective-permute-start.15
  83.0 1.6 %collective-permute-done.15.lo.refs_5_ = f32[8,6,4,128]{3,2,1,0:T(4,128)S(1)} collective-permute-done((f32[8,6,4,128]{3,2,1,0:T(4,128)S(1)}, f32[8,6,4,128]{3,2,1,0:T(4,128)S(1)}, u32[]{:S(2)}, u32[]{:S(2)}) %collective-permute-start.15) | collective-permute-done | bytes 98336 | tf_op jit(solution)/shard_map/ppermute | solution.py:636
  84.6 2.7 %collective-permute-done.16.hi.refs_7_ = f32[8,6,4,128]{3,2,1,0:T(4,128)S(1)} collective-permute-done((f32[8,6,4,128]{3,2,1,0:T(4,128)S(1)}, f32[8,6,4,128]{3,2,1,0:T(4,128)S(1)}, u32[]{:S(2)}, u32[]{:S(2)}) %collective-permute-start.16) | collective-permute-done | bytes 98336 | tf_op jit(solution)/shard_map/ppermute | solution.py:636
  87.3 0.1 shard_map.116
  87.4 0.1 collective-permute-start.17
  87.5 5.8 %collective-permute-start.18 = (f32[4,6,16,128]{3,2,1,0:T(8,128)S(1)}, f32[4,6,16,128]{3,2,1,0:T(8,128)S(1)}, u32[]{:S(2)}, u32[]{:S(2)}) collective-permute-start(f32[4,6,16,128]{3,2,1,0:T(8,128)S(1)} %get-tuple-element.57), channel_id=1, source_target_pairs={{0,248},{8,0},{16,8},{24,16},{32,24},{40,32},{48,40},{56,48},{64,5... | collective-permute-start | bytes 589832 | tf_op jit(solution)/shard_map/ppermute | solution.py:636
  93.2 4.6 %collective-permute-done.17.refs_8_ = f32[4,6,16,128]{3,2,1,0:T(8,128)S(1)} collective-permute-done((f32[4,6,16,128]{3,2,1,0:T(8,128)S(1)}, f32[4,6,16,128]{3,2,1,0:T(8,128)S(1)}, u32[]{:S(2)}, u32[]{:S(2)}) %collective-permute-start.17) | collective-permute-done | bytes 196640 | tf_op jit(solution)/shard_map/ppermute | solution.py:636
  97.8 10.8 %shard_map.117 = (f32[26,8,8,128]{3,2,1,0:T(8,128)S(1)}, f32[26,8,8,128]{3,2,1,0:T(8,128)S(1)}, f32[256,2,128]{2,1,0:T(2,128)S(1)}) custom-call(f32[26,8,8,128]{3,2,1,0:T(8,128)S(1)} %copy-done.1, f32[26,4,16,128]{3,2,1,0:T(8,128)S(1)} %collective-permute-done.2.refs_1_, f32[26,4,16,128]{3,2,1,0:T(8,128)S(1)} %collective-permute-done.3.refs_2_, ...), custom_call_target="tpu_custom_call" | custom-call | tf_op jit(solution)/shard_map/pallas_call | solution.py:708
  108.7 24.1 %all_to_all.5 = f32[256,2,128]{2,1,0:T(2,128)S(1)} all-to-all(f32[256,2,128]{2,1,0:T(2,128)S(1)} %get-tuple-element.61), channel_id=1, replica_groups=mesh['gx'=32,'st'=8] {'gx','st'}, dimensions={0} | all-to-all | bytes 524288 | tf_op jit(solution)/shard_map/all_to_all | solution.py:718
  132.8 5.0 %shard_map.118 = (f32[32,128]{1,0:T(8,128)}, f32[32,128]{1,0:T(8,128)}, f32[32,128]{1,0:T(8,128)}, f32[1,1]{1,0:T(1,128)}, f32[26,8,8,128]{3,2,1,0:T(8,128)}) custom-call(f32[1]{0:T(128)} %constant.5.clone.1.scale, f32[512,128]{1,0:T(8,128)S(1)} %bitcast.15, f32[32,128]{1,0:T(8,128)S(1)} %bitcast.12, f32[32,128]{1,0:T(8,128)S(1)} %bitcast.16, ...), custom_call_target="tpu_custom_call" | custom-call | tf_op jit(solution)/shard_map/pallas_call | solution.py:722
  (31 shorter events, 0.1 us)
Async XLA Ops:
  0.6 11.5 %copy-start = (f32[4096]{0:T(1024)S(1)}, f32[4096]{0:T(1024)}, u32[]{:S(2)}) copy-start(f32[4096]{0:T(1024)} %param.11) | copy-start | bytes 49156
  0.6 1.2 copy-start.2
  1.8 10.3 %copy-start.6 = (s32[8,8]{1,0:T(8,128)S(1)}, s32[8,8]{1,0:T(8,128)}, u32[]{:S(2)}) copy-start(s32[8,8]{1,0:T(8,128)} %param.10) | copy-start | bytes 772
  3.6 12.4 %collective-permute-start.6 = (f32[416,128]{1,0:T(8,128)}, f32[416,128]{1,0:T(8,128)S(1)}, u32[]{:S(2)}, u32[]{:S(2)}) collective-permute-start(f32[416,128]{1,0:T(8,128)} %get-tuple-element.42), channel_id=1, source_target_pairs={{0,3},{1,4},{2,5},{3,6},{4,7},{5,0},{6,1},{7,2},{8,11},{9,12},{10,... | collective-permute-start | bytes 638984 | tf_op jit(solution)/shard_map/ppermute | solution.py:636
  10.4 2.7 %copy-start.3 = (f32[26,1,64,128]{3,2,1,0:T(8,128)S(1)}, f32[26,1,64,128]{3,2,1,0:T(8,128)}, u32[]{:S(2)}) copy-start(f32[26,1,64,128]{3,2,1,0:T(8,128)} %param.7) | copy-start | bytes 2555908
  10.4 17.3 %collective-permute-start = (f32[26,8,4,128]{3,2,1,0:T(4,128)}, f32[26,8,4,128]{3,2,1,0:T(4,128)S(1)}, u32[]{:S(2)}, u32[]{:S(2)}) collective-permute-start(f32[26,8,4,128]{3,2,1,0:T(4,128)} %get-tuple-element.71), channel_id=1, source_target_pairs={{0,1},{1,2},{2,3},{3,4},{4,5},{5,6},{6,7},{7,0},{8,9},{9,10},{10,1... | collective-permute-start | bytes 1277960 | tf_op jit(solution)/shard_map/ppermute | solution.py:636
  12.1 5.5 %copy-start.1 = (f32[26,8,8,128]{3,2,1,0:T(8,128)S(1)}, f32[26,8,8,128]{3,2,1,0:T(8,128)}, u32[]{:S(2)}) copy-start(f32[26,8,8,128]{3,2,1,0:T(8,128)} %refs_0_.1) | copy-start | bytes 2555908
  13.7 11.5 %collective-permute-start.10 = (f32[480,128]{1,0:T(8,128)S(1)}, f32[480,128]{1,0:T(8,128)S(1)}, u32[]{:S(2)}, u32[]{:S(2)}) collective-permute-start(f32[480,128]{1,0:T(8,128)S(1)} %get-tuple-element.46), channel_id=1, source_target_pairs={{0,7},{1,0},{2,1},{3,2},{4,3},{5,4},{6,5},{7,6},{8,15},{9,8},{10,9... | collective-permute-start | bytes 737288 | tf_op jit(solution)/shard_map/ppermute | solution.py:636
  14.1 13.4 %collective-permute-start.4 = (f32[480,128]{1,0:T(8,128)S(1)}, f32[480,128]{1,0:T(8,128)S(1)}, u32[]{:S(2)}, u32[]{:S(2)}) collective-permute-start(f32[480,128]{1,0:T(8,128)S(1)} %get-tuple-element.40), channel_id=1, source_target_pairs={{0,1},{1,2},{2,3},{3,4},{4,5},{5,6},{6,7},{7,0},{8,9},{9,10},{10,1... | collective-permute-start | bytes 737288 | tf_op jit(solution)/shard_map/ppermute | solution.py:636
  15.4 8.7 %collective-permute-start.8 = (f32[416,128]{1,0:T(8,128)S(1)}, f32[416,128]{1,0:T(8,128)S(1)}, u32[]{:S(2)}, u32[]{:S(2)}) collective-permute-start(f32[416,128]{1,0:T(8,128)S(1)} %get-tuple-element.44), channel_id=1, source_target_pairs={{0,5},{1,6},{2,7},{3,0},{4,1},{5,2},{6,3},{7,4},{8,13},{9,14},{10,... | collective-permute-start | bytes 638984 | tf_op jit(solution)/shard_map/ppermute | solution.py:636
  16.0 13.1 %collective-permute-start.1 = (f32[26,8,4,128]{3,2,1,0:T(4,128)}, f32[26,8,4,128]{3,2,1,0:T(4,128)S(1)}, u32[]{:S(2)}, u32[]{:S(2)}) collective-permute-start(f32[26,8,4,128]{3,2,1,0:T(4,128)} %get-tuple-element.72), channel_id=1, source_target_pairs={{0,7},{1,0},{2,1},{3,2},{4,3},{5,4},{6,5},{7,6},{8,15},{9,8},{10,9... | collective-permute-start | bytes 1277960 | tf_op jit(solution)/shard_map/ppermute | solution.py:636
  24.2 13.4 %collective-permute-start.5 = (f32[416,128]{1,0:T(8,128)S(1)}, f32[416,128]{1,0:T(8,128)S(1)}, u32[]{:S(2)}, u32[]{:S(2)}) collective-permute-start(f32[416,128]{1,0:T(8,128)S(1)} %get-tuple-element.41), channel_id=1, source_target_pairs={{0,2},{1,3},{2,4},{3,5},{4,6},{5,7},{6,0},{7,1},{8,10},{9,11},{10,... | collective-permute-start | bytes 638984 | tf_op jit(solution)/shard_map/ppermute | solution.py:636
  25.1 12.6 %collective-permute-start.7 = (f32[416,128]{1,0:T(8,128)S(1)}, f32[416,128]{1,0:T(8,128)S(1)}, u32[]{:S(2)}, u32[]{:S(2)}) collective-permute-start(f32[416,128]{1,0:T(8,128)S(1)} %get-tuple-element.43), channel_id=1, source_target_pairs={{0,4},{1,5},{2,6},{3,7},{4,0},{5,1},{6,2},{7,3},{8,12},{9,13},{10,... | collective-permute-start | bytes 638984 | tf_op jit(solution)/shard_map/ppermute | solution.py:636
  27.5 16.5 %collective-permute-start.9 = (f32[416,128]{1,0:T(8,128)S(1)}, f32[416,128]{1,0:T(8,128)S(1)}, u32[]{:S(2)}, u32[]{:S(2)}) collective-permute-start(f32[416,128]{1,0:T(8,128)S(1)} %get-tuple-element.45), channel_id=1, source_target_pairs={{0,6},{1,7},{2,0},{3,1},{4,2},{5,3},{6,4},{7,5},{8,14},{9,15},{10,... | collective-permute-start | bytes 638984 | tf_op jit(solution)/shard_map/ppermute | solution.py:636
  27.7 18.7 %collective-permute-start.11 = (f32[960,128]{1,0:T(8,128)S(1)}, f32[960,128]{1,0:T(8,128)S(1)}, u32[]{:S(2)}, u32[]{:S(2)}) collective-permute-start(f32[960,128]{1,0:T(8,128)S(1)} %get-tuple-element.47), channel_id=1, source_target_pairs={{0,8},{8,16},{16,24},{24,32},{32,40},{40,48},{48,56},{56,64},{64,7... | collective-permute-start | bytes 1474568 | tf_op jit(solution)/shard_map/ppermute | solution.py:636
  29.3 68.5 %collective-permute-start.3 = (f32[26,4,16,128]{3,2,1,0:T(8,128)S(1)}, f32[26,4,16,128]{3,2,1,0:T(8,128)S(1)}, u32[]{:S(2)}, u32[]{:S(2)}) collective-permute-start(f32[26,4,16,128]{3,2,1,0:T(8,128)S(1)} %pad_maximum_fusion.1), channel_id=1, source_target_pairs={{0,248},{8,0},{16,8},{24,16},{32,24},{40,32},{48,40},{56,48},{64,5... | collective-permute-start | bytes 2555912 | tf_op jit(solution)/shard_map/ppermute | solution.py:636
  37.6 60.2 %collective-permute-start.2 = (f32[26,4,16,128]{3,2,1,0:T(8,128)S(1)}, f32[26,4,16,128]{3,2,1,0:T(8,128)S(1)}, u32[]{:S(2)}, u32[]{:S(2)}) collective-permute-start(f32[26,4,16,128]{3,2,1,0:T(8,128)S(1)} %pad_maximum_fusion), channel_id=1, source_target_pairs={{0,8},{8,16},{16,24},{24,32},{32,40},{40,48},{48,56},{56,64},{64,7... | collective-permute-start | bytes 2555912 | tf_op jit(solution)/shard_map/ppermute | solution.py:636
  37.7 29.0 %collective-permute-start.12 = (f32[960,128]{1,0:T(8,128)S(1)}, f32[960,128]{1,0:T(8,128)S(1)}, u32[]{:S(2)}, u32[]{:S(2)}) collective-permute-start(f32[960,128]{1,0:T(8,128)S(1)} %get-tuple-element.48), channel_id=1, source_target_pairs={{0,248},{8,0},{16,8},{24,16},{32,24},{40,32},{48,40},{56,48},{64,5... | collective-permute-start | bytes 1474568 | tf_op jit(solution)/shard_map/ppermute | solution.py:636
  44.3 29.5 %collective-permute-start.13 = (f32[832,128]{1,0:T(8,128)S(1)}, f32[832,128]{1,0:T(8,128)S(1)}, u32[]{:S(2)}, u32[]{:S(2)}) collective-permute-start(f32[832,128]{1,0:T(8,128)S(1)} %get-tuple-element.49), channel_id=1, source_target_pairs={{0,8},{8,16},{16,24},{24,32},{32,40},{40,48},{48,56},{56,64},{64,7... | collective-permute-start | bytes 1277960 | tf_op jit(solution)/shard_map/ppermute | solution.py:636
  46.4 29.2 %collective-permute-start.14 = (f32[832,128]{1,0:T(8,128)S(1)}, f32[832,128]{1,0:T(8,128)S(1)}, u32[]{:S(2)}, u32[]{:S(2)}) collective-permute-start(f32[832,128]{1,0:T(8,128)S(1)} %get-tuple-element.50), channel_id=1, source_target_pairs={{0,248},{8,0},{16,8},{24,16},{32,24},{40,32},{48,40},{56,48},{64,5... | collective-permute-start | bytes 1277960 | tf_op jit(solution)/shard_map/ppermute | solution.py:636
  82.3 2.3 %collective-permute-start.15 = (f32[8,6,4,128]{3,2,1,0:T(4,128)S(1)}, f32[8,6,4,128]{3,2,1,0:T(4,128)S(1)}, u32[]{:S(2)}, u32[]{:S(2)}) collective-permute-start(f32[8,6,4,128]{3,2,1,0:T(4,128)S(1)} %get-tuple-element.53), channel_id=1, source_target_pairs={{0,1},{1,2},{2,3},{3,4},{4,5},{5,6},{6,7},{7,0},{8,9},{9,10},{10,1... | collective-permute-start | bytes 294920 | tf_op jit(solution)/shard_map/ppermute | solution.py:636
  83.0 4.3 %collective-permute-start.16 = (f32[8,6,4,128]{3,2,1,0:T(4,128)S(1)}, f32[8,6,4,128]{3,2,1,0:T(4,128)S(1)}, u32[]{:S(2)}, u32[]{:S(2)}) collective-permute-start(f32[8,6,4,128]{3,2,1,0:T(4,128)S(1)} %get-tuple-element.55), channel_id=1, source_target_pairs={{0,7},{1,0},{2,1},{3,2},{4,3},{5,4},{6,5},{7,6},{8,15},{9,8},{10,9... | collective-permute-start | bytes 294920 | tf_op jit(solution)/shard_map/ppermute | solution.py:636
  87.4 10.4 %collective-permute-start.17 = (f32[4,6,16,128]{3,2,1,0:T(8,128)S(1)}, f32[4,6,16,128]{3,2,1,0:T(8,128)S(1)}, u32[]{:S(2)}, u32[]{:S(2)}) collective-permute-start(f32[4,6,16,128]{3,2,1,0:T(8,128)S(1)} %get-tuple-element.56), channel_id=1, source_target_pairs={{0,8},{8,16},{16,24},{24,32},{32,40},{40,48},{48,56},{56,64},{64,7... | collective-permute-start | bytes 589832 | tf_op jit(solution)/shard_map/ppermute | solution.py:636
  87.5 10.3 %collective-permute-start.18 = (f32[4,6,16,128]{3,2,1,0:T(8,128)S(1)}, f32[4,6,16,128]{3,2,1,0:T(8,128)S(1)}, u32[]{:S(2)}, u32[]{:S(2)}) collective-permute-start(f32[4,6,16,128]{3,2,1,0:T(8,128)S(1)} %get-tuple-element.57), channel_id=1, source_target_pairs={{0,248},{8,0},{16,8},{24,16},{32,24},{40,32},{48,40},{56,48},{64,5... | collective-permute-start | bytes 589832 | tf_op jit(solution)/shard_map/ppermute | solution.py:636
  97.8 35.0 %copy-start.4 = (f32[4096]{0:T(1024)S(1)}, f32[4096]{0:T(1024)}, u32[]{:S(2)}) copy-start(f32[4096]{0:T(1024)} %param.12) | copy-start | bytes 49156
  97.8 35.0 %copy-start.5 = (f32[4096]{0:T(1024)S(1)}, f32[4096]{0:T(1024)}, u32[]{:S(2)}) copy-start(f32[4096]{0:T(1024)} %param.13) | copy-start | bytes 49156

commit v2 on v1

--- a/solution.py
+++ b/solution.py
@@ -659,7 +659,7 @@
     )(place, plane, flags)
 
     planes = [packed[0]] + [None] * 7
-    for k in (5, 3, 1, 7, 2, 6, 4):
+    for k in (2, 6, 4, 5, 3, 1, 7):
         planes[k] = neighbour(packed[k], "st", k)
 
     def both(value, axis):
@@ -668,19 +668,19 @@
         high = neighbour(high, axis, -1)
         return low, high
 
-    halos = []
+    sent = call(route_second_kernel, [(2 * LINES, DEPTH)] * 2, (), 8, in_specs=smem + [on_chip] * 4)(
+        place, planes[0], planes[4], planes[2], planes[6]
+    )
+    others = both(sent, "gx")
     lines = 2 * LINES + PLANE_FLAGS
     sent = call(route_first_kernel, [(lines, DEPTH)] * 2, (), 8, in_specs=smem + [on_chip] * 5)(
         place, planes[1], planes[5], planes[3], planes[7], flags
     )
-    halos += both(sent, "gx")
+    halos = both(sent, "gx")
     region, table = call(table_kernel, [(2, WIDE, WIDE, DEPTH), (WIDE, 20, WIDE, DEPTH)], mib=8)(
         planes[1], planes[7], flags, *halos
     )
-    sent = call(route_second_kernel, [(2 * LINES, DEPTH)] * 2, (), 8, in_specs=smem + [on_chip] * 4)(
-        place, planes[0], planes[4], planes[2], planes[6]
-    )
-    halos += both(sent, "gx")
+    halos += others
 
     slo, shi = both((adjoint_in[:, :, 4:8], adjoint_in[:, :, 0:4]), "st")
 

time: 138 us -> 138 us (level)
  no operation moved by 1% of the time
where the time goes in v2:
time: 138 us
  waiting for transfers between devices  42.7 us (31%)
  starting transfers between devices  36.8 us (27%)
  Pallas kernels  26.5 us (19%)
  blocking collectives  24.1 us (17%)
  local copies, waits for them, and re-layouts  4.89 us (4%)
  other arithmetic  1.89 us (1%)
    ppermute x19, waiting for transfers between devices, neighbour(): lax.ppermute(value, axis, [(i, (i + step) % count) for i in range(count)])  42.7 us
    ppermute x19, starting transfers between devices, neighbour(): lax.ppermute(value, axis, [(i, (i + step) % count) for i in range(count)])  36.8 us
    all_to_all x1, blocking collectives, window(): told = lax.all_to_all(slots, ('gx', 'st'), 0, 0, tiled=True)  24.1 us
    pallas_call x1, Pallas kernels, window(): call(backward_kernel, [mine, mine, (count, 2, DEPTH)], [vmem(big, f32)] *...  10.8 us
    pallas_call x1, Pallas kernels, window(): call(forward_kernel, [(3, WIDE, 4, WIDE, DEPTH), (OWN, 6, OWN, DEPTH), (O...  6.69 us
    pallas_call x1, Pallas kernels, window(): call(tile_kernel, [tiles] * 3 + [(1, 1), mine], [vmem(mine, f32)] * 2 + [...  4.98 us
  transfers between devices with their start and end apart: 19, of which 8 were waited for; matrix products, arithmetic and copies ran while one was open for 4% of the time, Pallas kernels for 6%

profile of v2, /device:TPU:1, one launch (start us, length us, event | category | flops | bytes accessed | tf_op | source)
XLA Modules:
  0.0 138.0 jit_solution(15218117079801167730)
XLA Ops:
  0.6 0.0 copy-start.2
  0.7 1.1 copy-done.2
  1.8 1.8 %shard_map.110 = (f32[416,128]{1,0:T(8,128)S(1)}, f32[416,128]{1,0:T(8,128)S(1)}, f32[416,128]{1,0:T(8,128)}, f32[416,128]{1,0:T(8,128)S(1)}, f32[416,128]{1,0:T(8,128)S(1)}, /*index=5*/f32[416,128]{1,0:T(8,128)S(1)}) custom-call(s32[1]{0:T(128)} %bitcast.place, f32[26,64,128]{2,1,0:T(8,128)S(1)} %bitcast.13), custom_call_target="tpu_custom_call" | custom-call | tf_op jit(solution)/shard_map/pallas_call | solution.py:650
  3.6 4.3 %collective-permute-start.6 = (f32[416,128]{1,0:T(8,128)}, f32[416,128]{1,0:T(8,128)S(1)}, u32[]{:S(2)}, u32[]{:S(2)}) collective-permute-start(f32[416,128]{1,0:T(8,128)} %get-tuple-element.42), channel_id=1, source_target_pairs={{0,3},{1,4},{2,5},{3,6},{4,7},{5,0},{6,1},{7,2},{8,11},{9,12},{10,... | collective-permute-start | bytes 638984 | tf_op jit(solution)/shard_map/ppermute | solution.py:636
  7.9 2.5 %fusion.1 = (f32[26,8,4,128]{3,2,1,0:T(4,128)}, f32[26,8,4,128]{3,2,1,0:T(4,128)}) fusion(f32[26,8,8,128]{3,2,1,0:T(8,128)} %refs_0_.1), kind=kLoop, calls=%fused_computation.8 | loop fusion | bytes 1703936 | tf_op jit(solution)/shard_map/slice | solution.py:685
  10.4 0.8 compare_select_fusion
  11.2 0.1 reshape.62
  11.3 0.8 convert_bitcast_fusion
  12.1 0.0 copy-start.1
  12.1 0.8 gather_fusion
  12.9 0.1 reshape.61
  13.0 0.1 convert_element_type.21
  13.1 0.1 stack_broadcast_in_dim.2
  13.1 0.5 shard_map.111
  13.7 0.4 collective-permute-start.10
  14.1 1.3 collective-permute-start.4
  15.4 0.6 collective-permute-start.8
  16.0 1.6 %collective-permute-start.1 = (f32[26,8,4,128]{3,2,1,0:T(4,128)}, f32[26,8,4,128]{3,2,1,0:T(4,128)S(1)}, u32[]{:S(2)}, u32[]{:S(2)}) collective-permute-start(f32[26,8,4,128]{3,2,1,0:T(4,128)} %get-tuple-element.72), channel_id=1, source_target_pairs={{0,7},{1,0},{2,1},{3,2},{4,3},{5,4},{6,5},{7,6},{8,15},{9,8},{10,9... | collective-permute-start | bytes 1277960 | tf_op jit(solution)/shard_map/ppermute | solution.py:636
  17.6 0.1 fusion
  17.6 6.5 %collective-permute-done.8.b.refs_5_ = f32[416,128]{1,0:T(8,128)S(1)} collective-permute-done((f32[416,128]{1,0:T(8,128)S(1)}, f32[416,128]{1,0:T(8,128)S(1)}, u32[]{:S(2)}, u32[]{:S(2)}) %collective-permute-start.8) | collective-permute-done | bytes 213024 | tf_op jit(solution)/shard_map/ppermute | solution.py:636
  24.2 1.0 collective-permute-start.5
  25.1 2.4 %collective-permute-start.7 = (f32[416,128]{1,0:T(8,128)S(1)}, f32[416,128]{1,0:T(8,128)S(1)}, u32[]{:S(2)}, u32[]{:S(2)}) collective-permute-start(f32[416,128]{1,0:T(8,128)S(1)} %get-tuple-element.43), channel_id=1, source_target_pairs={{0,4},{1,5},{2,6},{3,7},{4,0},{5,1},{6,2},{7,3},{8,12},{9,13},{10,... | collective-permute-start | bytes 638984 | tf_op jit(solution)/shard_map/ppermute | solution.py:636
  27.5 0.2 shard_map.112
  27.7 1.3 collective-permute-start.11
  29.1 0.2 pad_maximum_fusion.1
  29.3 8.1 %collective-permute-start.3 = (f32[26,4,16,128]{3,2,1,0:T(8,128)S(1)}, f32[26,4,16,128]{3,2,1,0:T(8,128)S(1)}, u32[]{:S(2)}, u32[]{:S(2)}) collective-permute-start(f32[26,4,16,128]{3,2,1,0:T(8,128)S(1)} %pad_maximum_fusion.1), channel_id=1, source_target_pairs={{0,248},{8,0},{16,8},{24,16},{32,24},{40,32},{48,40},{56,48},{64,5... | collective-permute-start | bytes 2555912 | tf_op jit(solution)/shard_map/ppermute | solution.py:636
  37.4 0.2 pad_maximum_fusion
  37.6 0.1 collective-permute-start.2
  37.7 6.4 %collective-permute-start.12 = (f32[960,128]{1,0:T(8,128)S(1)}, f32[960,128]{1,0:T(8,128)S(1)}, u32[]{:S(2)}, u32[]{:S(2)}) collective-permute-start(f32[960,128]{1,0:T(8,128)S(1)} %get-tuple-element.48), channel_id=1, source_target_pairs={{0,248},{8,0},{16,8},{24,16},{32,24},{40,32},{48,40},{56,48},{64,5... | collective-permute-start | bytes 1474568 | tf_op jit(solution)/shard_map/ppermute | solution.py:636
  44.1 0.2 shard_map.113
  44.3 0.1 collective-permute-start.13
  44.3 2.1 %collective-permute-done.11.from_left.refs_8_ = f32[960,128]{1,0:T(8,128)S(1)} collective-permute-done((f32[960,128]{1,0:T(8,128)S(1)}, f32[960,128]{1,0:T(8,128)S(1)}, u32[]{:S(2)}, u32[]{:S(2)}) %collective-permute-start.11) | collective-permute-done | bytes 491552 | tf_op jit(solution)/shard_map/ppermute | solution.py:636
  46.4 2.7 %collective-permute-start.14 = (f32[832,128]{1,0:T(8,128)S(1)}, f32[832,128]{1,0:T(8,128)S(1)}, u32[]{:S(2)}, u32[]{:S(2)}) collective-permute-start(f32[832,128]{1,0:T(8,128)S(1)} %get-tuple-element.50), channel_id=1, source_target_pairs={{0,248},{8,0},{16,8},{24,16},{32,24},{40,32},{48,40},{56,48},{64,5... | collective-permute-start | bytes 1277960 | tf_op jit(solution)/shard_map/ppermute | solution.py:636
  49.1 17.6 %collective-permute-done.12.from_right.refs_9_ = f32[960,128]{1,0:T(8,128)S(1)} collective-permute-done((f32[960,128]{1,0:T(8,128)S(1)}, f32[960,128]{1,0:T(8,128)S(1)}, u32[]{:S(2)}, u32[]{:S(2)}) %collective-permute-start.12) | collective-permute-done | bytes 491552 | tf_op jit(solution)/shard_map/ppermute | solution.py:636
  66.7 1.3 shard_map.114
  68.0 5.8 %collective-permute-done.13.refs_10_ = f32[832,128]{1,0:T(8,128)S(1)} collective-permute-done((f32[832,128]{1,0:T(8,128)S(1)}, f32[832,128]{1,0:T(8,128)S(1)}, u32[]{:S(2)}, u32[]{:S(2)}) %collective-permute-start.13) | collective-permute-done | bytes 426016 | tf_op jit(solution)/shard_map/ppermute | solution.py:636
  73.8 1.8 %collective-permute-done.14.refs_11_ = f32[832,128]{1,0:T(8,128)S(1)} collective-permute-done((f32[832,128]{1,0:T(8,128)S(1)}, f32[832,128]{1,0:T(8,128)S(1)}, u32[]{:S(2)}, u32[]{:S(2)}) %collective-permute-start.14) | collective-permute-done | bytes 426016 | tf_op jit(solution)/shard_map/ppermute | solution.py:636
  75.6 6.7 %shard_map.115 = (f32[3,16,4,16,128]{4,3,2,1,0:T(8,128)S(1)}, f32[8,6,8,128]{3,2,1,0:T(8,128)S(1)}, f32[8,6,4,128]{3,2,1,0:T(4,128)S(1)}, f32[8,6,4,128]{3,2,1,0:T(4,128)S(1)}, f32[1,128]{1,0:T(1,128)S(1)}) custom-call(s32[1]{0:T(128)} %bitcast.place, f32[416,128]{1,0:T(8,128)S(1)} %get-tuple-element.37.a.refs_0_, ...), custom_call_target="tpu_custom_call" | custom-call | tf_op jit(solution)/shard_map/pallas_call | solution.py:694
  82.3 0.7 collective-permute-start.15
  83.0 1.6 %collective-permute-done.15.lo.refs_5_ = f32[8,6,4,128]{3,2,1,0:T(4,128)S(1)} collective-permute-done((f32[8,6,4,128]{3,2,1,0:T(4,128)S(1)}, f32[8,6,4,128]{3,2,1,0:T(4,128)S(1)}, u32[]{:S(2)}, u32[]{:S(2)}) %collective-permute-start.15) | collective-permute-done | bytes 98336 | tf_op jit(solution)/shard_map/ppermute | solution.py:636
  84.6 2.7 %collective-permute-done.16.hi.refs_7_ = f32[8,6,4,128]{3,2,1,0:T(4,128)S(1)} collective-permute-done((f32[8,6,4,128]{3,2,1,0:T(4,128)S(1)}, f32[8,6,4,128]{3,2,1,0:T(4,128)S(1)}, u32[]{:S(2)}, u32[]{:S(2)}) %collective-permute-start.16) | collective-permute-done | bytes 98336 | tf_op jit(solution)/shard_map/ppermute | solution.py:636
  87.3 0.1 shard_map.116
  87.4 0.1 collective-permute-start.17
  87.5 5.8 %collective-permute-start.18 = (f32[4,6,16,128]{3,2,1,0:T(8,128)S(1)}, f32[4,6,16,128]{3,2,1,0:T(8,128)S(1)}, u32[]{:S(2)}, u32[]{:S(2)}) collective-permute-start(f32[4,6,16,128]{3,2,1,0:T(8,128)S(1)} %get-tuple-element.57), channel_id=1, source_target_pairs={{0,248},{8,0},{16,8},{24,16},{32,24},{40,32},{48,40},{56,48},{64,5... | collective-permute-start | bytes 589832 | tf_op jit(solution)/shard_map/ppermute | solution.py:636
  93.2 4.6 %collective-permute-done.17.refs_8_ = f32[4,6,16,128]{3,2,1,0:T(8,128)S(1)} collective-permute-done((f32[4,6,16,128]{3,2,1,0:T(8,128)S(1)}, f32[4,6,16,128]{3,2,1,0:T(8,128)S(1)}, u32[]{:S(2)}, u32[]{:S(2)}) %collective-permute-start.17) | collective-permute-done | bytes 196640 | tf_op jit(solution)/shard_map/ppermute | solution.py:636
  97.8 10.8 %shard_map.117 = (f32[26,8,8,128]{3,2,1,0:T(8,128)S(1)}, f32[26,8,8,128]{3,2,1,0:T(8,128)S(1)}, f32[256,2,128]{2,1,0:T(2,128)S(1)}) custom-call(f32[26,8,8,128]{3,2,1,0:T(8,128)S(1)} %copy-done.1, f32[26,4,16,128]{3,2,1,0:T(8,128)S(1)} %collective-permute-done.2.refs_1_, f32[26,4,16,128]{3,2,1,0:T(8,128)S(1)} %collective-permute-done.3.refs_2_, ...), custom_call_target="tpu_custom_call" | custom-call | tf_op jit(solution)/shard_map/pallas_call | solution.py:708
  108.7 24.1 %all_to_all.5 = f32[256,2,128]{2,1,0:T(2,128)S(1)} all-to-all(f32[256,2,128]{2,1,0:T(2,128)S(1)} %get-tuple-element.61), channel_id=1, replica_groups=mesh['gx'=32,'st'=8] {'gx','st'}, dimensions={0} | all-to-all | bytes 524288 | tf_op jit(solution)/shard_map/all_to_all | solution.py:718
  132.8 5.0 %shard_map.118 = (f32[32,128]{1,0:T(8,128)}, f32[32,128]{1,0:T(8,128)}, f32[32,128]{1,0:T(8,128)}, f32[1,1]{1,0:T(1,128)}, f32[26,8,8,128]{3,2,1,0:T(8,128)}) custom-call(f32[1]{0:T(128)} %constant.5.clone.1.scale, f32[512,128]{1,0:T(8,128)S(1)} %bitcast.15, f32[32,128]{1,0:T(8,128)S(1)} %bitcast.12, f32[32,128]{1,0:T(8,128)S(1)} %bitcast.16, ...), custom_call_target="tpu_custom_call" | custom-call | tf_op jit(solution)/shard_map/pallas_call | solution.py:722
  (31 shorter events, 0.1 us)
Async XLA Ops:
  0.6 11.5 %copy-start = (f32[4096]{0:T(1024)S(1)}, f32[4096]{0:T(1024)}, u32[]{:S(2)}) copy-start(f32[4096]{0:T(1024)} %param.11) | copy-start | bytes 49156
  0.6 1.2 copy-start.2
  1.8 10.3 %copy-start.6 = (s32[8,8]{1,0:T(8,128)S(1)}, s32[8,8]{1,0:T(8,128)}, u32[]{:S(2)}) copy-start(s32[8,8]{1,0:T(8,128)} %param.10) | copy-start | bytes 772
  3.6 12.4 %collective-permute-start.6 = (f32[416,128]{1,0:T(8,128)}, f32[416,128]{1,0:T(8,128)S(1)}, u32[]{:S(2)}, u32[]{:S(2)}) collective-permute-start(f32[416,128]{1,0:T(8,128)} %get-tuple-element.42), channel_id=1, source_target_pairs={{0,3},{1,4},{2,5},{3,6},{4,7},{5,0},{6,1},{7,2},{8,11},{9,12},{10,... | collective-permute-start | bytes 638984 | tf_op jit(solution)/shard_map/ppermute | solution.py:636
  10.4 2.7 %copy-start.3 = (f32[26,1,64,128]{3,2,1,0:T(8,128)S(1)}, f32[26,1,64,128]{3,2,1,0:T(8,128)}, u32[]{:S(2)}) copy-start(f32[26,1,64,128]{3,2,1,0:T(8,128)} %param.7) | copy-start | bytes 2555908
  10.4 17.3 %collective-permute-start = (f32[26,8,4,128]{3,2,1,0:T(4,128)}, f32[26,8,4,128]{3,2,1,0:T(4,128)S(1)}, u32[]{:S(2)}, u32[]{:S(2)}) collective-permute-start(f32[26,8,4,128]{3,2,1,0:T(4,128)} %get-tuple-element.71), channel_id=1, source_target_pairs={{0,1},{1,2},{2,3},{3,4},{4,5},{5,6},{6,7},{7,0},{8,9},{9,10},{10,1... | collective-permute-start | bytes 1277960 | tf_op jit(solution)/shard_map/ppermute | solution.py:636
  12.1 5.5 %copy-start.1 = (f32[26,8,8,128]{3,2,1,0:T(8,128)S(1)}, f32[26,8,8,128]{3,2,1,0:T(8,128)}, u32[]{:S(2)}) copy-start(f32[26,8,8,128]{3,2,1,0:T(8,128)} %refs_0_.1) | copy-start | bytes 2555908
  13.7 11.5 %collective-permute-start.10 = (f32[480,128]{1,0:T(8,128)S(1)}, f32[480,128]{1,0:T(8,128)S(1)}, u32[]{:S(2)}, u32[]{:S(2)}) collective-permute-start(f32[480,128]{1,0:T(8,128)S(1)} %get-tuple-element.46), channel_id=1, source_target_pairs={{0,7},{1,0},{2,1},{3,2},{4,3},{5,4},{6,5},{7,6},{8,15},{9,8},{10,9... | collective-permute-start | bytes 737288 | tf_op jit(solution)/shard_map/ppermute | solution.py:636
  14.1 13.4 %collective-permute-start.4 = (f32[480,128]{1,0:T(8,128)S(1)}, f32[480,128]{1,0:T(8,128)S(1)}, u32[]{:S(2)}, u32[]{:S(2)}) collective-permute-start(f32[480,128]{1,0:T(8,128)S(1)} %get-tuple-element.40), channel_id=1, source_target_pairs={{0,1},{1,2},{2,3},{3,4},{4,5},{5,6},{6,7},{7,0},{8,9},{9,10},{10,1... | collective-permute-start | bytes 737288 | tf_op jit(solution)/shard_map/ppermute | solution.py:636
  15.4 8.7 %collective-permute-start.8 = (f32[416,128]{1,0:T(8,128)S(1)}, f32[416,128]{1,0:T(8,128)S(1)}, u32[]{:S(2)}, u32[]{:S(2)}) collective-permute-start(f32[416,128]{1,0:T(8,128)S(1)} %get-tuple-element.44), channel_id=1, source_target_pairs={{0,5},{1,6},{2,7},{3,0},{4,1},{5,2},{6,3},{7,4},{8,13},{9,14},{10,... | collective-permute-start | bytes 638984 | tf_op jit(solution)/shard_map/ppermute | solution.py:636
  16.0 13.1 %collective-permute-start.1 = (f32[26,8,4,128]{3,2,1,0:T(4,128)}, f32[26,8,4,128]{3,2,1,0:T(4,128)S(1)}, u32[]{:S(2)}, u32[]{:S(2)}) collective-permute-start(f32[26,8,4,128]{3,2,1,0:T(4,128)} %get-tuple-element.72), channel_id=1, source_target_pairs={{0,7},{1,0},{2,1},{3,2},{4,3},{5,4},{6,5},{7,6},{8,15},{9,8},{10,9... | collective-permute-start | bytes 1277960 | tf_op jit(solution)/shard_map/ppermute | solution.py:636
  24.2 13.4 %collective-permute-start.5 = (f32[416,128]{1,0:T(8,128)S(1)}, f32[416,128]{1,0:T(8,128)S(1)}, u32[]{:S(2)}, u32[]{:S(2)}) collective-permute-start(f32[416,128]{1,0:T(8,128)S(1)} %get-tuple-element.41), channel_id=1, source_target_pairs={{0,2},{1,3},{2,4},{3,5},{4,6},{5,7},{6,0},{7,1},{8,10},{9,11},{10,... | collective-permute-start | bytes 638984 | tf_op jit(solution)/shard_map/ppermute | solution.py:636
  25.1 12.6 %collective-permute-start.7 = (f32[416,128]{1,0:T(8,128)S(1)}, f32[416,128]{1,0:T(8,128)S(1)}, u32[]{:S(2)}, u32[]{:S(2)}) collective-permute-start(f32[416,128]{1,0:T(8,128)S(1)} %get-tuple-element.43), channel_id=1, source_target_pairs={{0,4},{1,5},{2,6},{3,7},{4,0},{5,1},{6,2},{7,3},{8,12},{9,13},{10,... | collective-permute-start | bytes 638984 | tf_op jit(solution)/shard_map/ppermute | solution.py:636
  27.5 16.5 %collective-permute-start.9 = (f32[416,128]{1,0:T(8,128)S(1)}, f32[416,128]{1,0:T(8,128)S(1)}, u32[]{:S(2)}, u32[]{:S(2)}) collective-permute-start(f32[416,128]{1,0:T(8,128)S(1)} %get-tuple-element.45), channel_id=1, source_target_pairs={{0,6},{1,7},{2,0},{3,1},{4,2},{5,3},{6,4},{7,5},{8,14},{9,15},{10,... | collective-permute-start | bytes 638984 | tf_op jit(solution)/shard_map/ppermute | solution.py:636
  27.7 18.7 %collective-permute-start.11 = (f32[960,128]{1,0:T(8,128)S(1)}, f32[960,128]{1,0:T(8,128)S(1)}, u32[]{:S(2)}, u32[]{:S(2)}) collective-permute-start(f32[960,128]{1,0:T(8,128)S(1)} %get-tuple-element.47), channel_id=1, source_target_pairs={{0,8},{8,16},{16,24},{24,32},{32,40},{40,48},{48,56},{56,64},{64,7... | collective-permute-start | bytes 1474568 | tf_op jit(solution)/shard_map/ppermute | solution.py:636
  29.3 68.5 %collective-permute-start.3 = (f32[26,4,16,128]{3,2,1,0:T(8,128)S(1)}, f32[26,4,16,128]{3,2,1,0:T(8,128)S(1)}, u32[]{:S(2)}, u32[]{:S(2)}) collective-permute-start(f32[26,4,16,128]{3,2,1,0:T(8,128)S(1)} %pad_maximum_fusion.1), channel_id=1, source_target_pairs={{0,248},{8,0},{16,8},{24,16},{32,24},{40,32},{48,40},{56,48},{64,5... | collective-permute-start | bytes 2555912 | tf_op jit(solution)/shard_map/ppermute | solution.py:636
  37.6 60.2 %collective-permute-start.2 = (f32[26,4,16,128]{3,2,1,0:T(8,128)S(1)}, f32[26,4,16,128]{3,2,1,0:T(8,128)S(1)}, u32[]{:S(2)}, u32[]{:S(2)}) collective-permute-start(f32[26,4,16,128]{3,2,1,0:T(8,128)S(1)} %pad_maximum_fusion), channel_id=1, source_target_pairs={{0,8},{8,16},{16,24},{24,32},{32,40},{40,48},{48,56},{56,64},{64,7... | collective-permute-start | bytes 2555912 | tf_op jit(solution)/shard_map/ppermute | solution.py:636
  37.7 29.0 %collective-permute-start.12 = (f32[960,128]{1,0:T(8,128)S(1)}, f32[960,128]{1,0:T(8,128)S(1)}, u32[]{:S(2)}, u32[]{:S(2)}) collective-permute-start(f32[960,128]{1,0:T(8,128)S(1)} %get-tuple-element.48), channel_id=1, source_target_pairs={{0,248},{8,0},{16,8},{24,16},{32,24},{40,32},{48,40},{56,48},{64,5... | collective-permute-start | bytes 1474568 | tf_op jit(solution)/shard_map/ppermute | solution.py:636
  44.3 29.5 %collective-permute-start.13 = (f32[832,128]{1,0:T(8,128)S(1)}, f32[832,128]{1,0:T(8,128)S(1)}, u32[]{:S(2)}, u32[]{:S(2)}) collective-permute-start(f32[832,128]{1,0:T(8,128)S(1)} %get-tuple-element.49), channel_id=1, source_target_pairs={{0,8},{8,16},{16,24},{24,32},{32,40},{40,48},{48,56},{56,64},{64,7... | collective-permute-start | bytes 1277960 | tf_op jit(solution)/shard_map/ppermute | solution.py:636
  46.4 29.2 %collective-permute-start.14 = (f32[832,128]{1,0:T(8,128)S(1)}, f32[832,128]{1,0:T(8,128)S(1)}, u32[]{:S(2)}, u32[]{:S(2)}) collective-permute-start(f32[832,128]{1,0:T(8,128)S(1)} %get-tuple-element.50), channel_id=1, source_target_pairs={{0,248},{8,0},{16,8},{24,16},{32,24},{40,32},{48,40},{56,48},{64,5... | collective-permute-start | bytes 1277960 | tf_op jit(solution)/shard_map/ppermute | solution.py:636
  82.3 2.3 %collective-permute-start.15 = (f32[8,6,4,128]{3,2,1,0:T(4,128)S(1)}, f32[8,6,4,128]{3,2,1,0:T(4,128)S(1)}, u32[]{:S(2)}, u32[]{:S(2)}) collective-permute-start(f32[8,6,4,128]{3,2,1,0:T(4,128)S(1)} %get-tuple-element.53), channel_id=1, source_target_pairs={{0,1},{1,2},{2,3},{3,4},{4,5},{5,6},{6,7},{7,0},{8,9},{9,10},{10,1... | collective-permute-start | bytes 294920 | tf_op jit(solution)/shard_map/ppermute | solution.py:636
  83.0 4.3 %collective-permute-start.16 = (f32[8,6,4,128]{3,2,1,0:T(4,128)S(1)}, f32[8,6,4,128]{3,2,1,0:T(4,128)S(1)}, u32[]{:S(2)}, u32[]{:S(2)}) collective-permute-start(f32[8,6,4,128]{3,2,1,0:T(4,128)S(1)} %get-tuple-element.55), channel_id=1, source_target_pairs={{0,7},{1,0},{2,1},{3,2},{4,3},{5,4},{6,5},{7,6},{8,15},{9,8},{10,9... | collective-permute-start | bytes 294920 | tf_op jit(solution)/shard_map/ppermute | solution.py:636
  87.4 10.4 %collective-permute-start.17 = (f32[4,6,16,128]{3,2,1,0:T(8,128)S(1)}, f32[4,6,16,128]{3,2,1,0:T(8,128)S(1)}, u32[]{:S(2)}, u32[]{:S(2)}) collective-permute-start(f32[4,6,16,128]{3,2,1,0:T(8,128)S(1)} %get-tuple-element.56), channel_id=1, source_target_pairs={{0,8},{8,16},{16,24},{24,32},{32,40},{40,48},{48,56},{56,64},{64,7... | collective-permute-start | bytes 589832 | tf_op jit(solution)/shard_map/ppermute | solution.py:636
  87.5 10.3 %collective-permute-start.18 = (f32[4,6,16,128]{3,2,1,0:T(8,128)S(1)}, f32[4,6,16,128]{3,2,1,0:T(8,128)S(1)}, u32[]{:S(2)}, u32[]{:S(2)}) collective-permute-start(f32[4,6,16,128]{3,2,1,0:T(8,128)S(1)} %get-tuple-element.57), channel_id=1, source_target_pairs={{0,248},{8,0},{16,8},{24,16},{32,24},{40,32},{48,40},{56,48},{64,5... | collective-permute-start | bytes 589832 | tf_op jit(solution)/shard_map/ppermute | solution.py:636
  97.8 35.0 %copy-start.4 = (f32[4096]{0:T(1024)S(1)}, f32[4096]{0:T(1024)}, u32[]{:S(2)}) copy-start(f32[4096]{0:T(1024)} %param.12) | copy-start | bytes 49156
  97.8 35.0 %copy-start.5 = (f32[4096]{0:T(1024)S(1)}, f32[4096]{0:T(1024)}, u32[]{:S(2)}) copy-start(f32[4096]{0:T(1024)} %param.13) | copy-start | bytes 49156

commit v3 on v1

--- a/solution.py
+++ b/solution.py
@@ -457,24 +457,26 @@
     loop(OWN + 2 * k, one)
 
 
-def backward_kernel(*refs):
-    own, gl, gr, slo, shi, elo, emid, ehi, el, er, mom, table, region, names, heat = refs[:15]
-    out_a, out_b, slots, la0, la1, lb0, lb1, late, sums, last_a, last_b, sems = refs[15:]
-
+def collect_kernel(own, gl, gr, slo, shi, lam):
     def gather(x):
         for i in range(26):
-            la0[x + HALO, i, 0:4] = slo[i, x]
-            la0[x + HALO, i, 4:12] = own[i, x]
-            la0[x + HALO, i, 12:16] = shi[i, x]
+            lam[x + HALO, i, 0:4] = slo[i, x]
+            lam[x + HALO, i, 4:12] = own[i, x]
+            lam[x + HALO, i, 12:16] = shi[i, x]
 
     loop(OWN, gather)
 
     def beside(x):
         for i in range(26):
-            la0[x, i] = gl[i, x]
-            la0[x + HALO + OWN, i] = gr[i, x]
+            lam[x, i] = gl[i, x]
+            lam[x + HALO + OWN, i] = gr[i, x]
 
     loop(HALO, beside)
+
+
+def backward_kernel(*refs):
+    start, elo, emid, ehi, el, er, mom, table, region, names, heat = refs[:11]
+    out_a, out_b, slots, la0, la1, lb0, lb1, late, sums, last_a, last_b, sems = refs[11:]
 
     def settle(x):
         for a in range(6):
@@ -508,7 +510,7 @@
             spot = pl.ds(OWN * OWN * chain + OWN * n, OWN)
             sums[spot] = value if fresh else sums[spot] + value
 
-    bufs = [(la0, la1), (lb0, lb1)]
+    bufs = [(start, la1), (lb0, lb1)]
     for k in (3, 2, 1, 0):
         for chain, (src, _) in enumerate(bufs):
             collect(chain, src, k == 3)
@@ -523,7 +525,7 @@
             return late[x, a] if k == 3 else mom[k, x, a]
 
         adjoint_planes(k, state_of, [src for src, _ in bufs], table, region, put)
-        bufs = [(dst, src) for src, dst in bufs]
+        bufs = [(dst, la0 if src is start else src) for src, dst in bufs]
     copies = [
         pltpu.make_async_copy(last_a, out_a, sems.at[0]),
         pltpu.make_async_copy(last_b, out_b, sems.at[1]),
@@ -703,6 +705,8 @@
     head, tail = call(merge_kernel, [(HALO, 6, WIDE, DEPTH)] * 2, mib=4)(elo, edge, ehi)
     el, er = both((tail, head), "gx")
 
+    lam = call(collect_kernel, [big], mib=4)(adjoint_in, gl, gr, slo, shi)[0]
+
     count = lax.axis_size("gx") * lax.axis_size("st")
     mine = (26, OWN, OWN, DEPTH)
     out_a, out_b, slots = call(
@@ -714,7 +718,7 @@
         + [pltpu.SemaphoreType.DMA((2,))],
         24,
         out_specs=[pltpu.HBM, pltpu.HBM, pltpu.VMEM],
-    )(adjoint_in, gl, gr, slo, shi, elo, edge, ehi, el, er, mom, table, region, names, heat)
+    )(lam, elo, edge, ehi, el, er, mom, table, region, names, heat)
     told = lax.all_to_all(slots, ("gx", "st"), 0, 0, tiled=True)
 
     scale = jnp.full((1,), 1.0 / (KAPPA * count * OWN * OWN), f32)

time: 138 us -> 138 us (level)
  transfers between devices with their start and end apart: 19 -> 19, of which waited for: 8 -> 8; matrix products, arithmetic and copies ran while one was open for 4% -> 4% of each run, Pallas kernels for 6% -> 7%
where the time goes in v3:
time: 138 us
  waiting for transfers between devices  42.2 us (31%)
  starting transfers between devices  36.8 us (27%)
  Pallas kernels  26.6 us (19%)
  blocking collectives  24.1 us (17%)
  local copies, waits for them, and re-layouts  4.88 us (4%)
  other arithmetic  1.87 us (1%)
    ppermute x19, waiting for transfers between devices, neighbour(): lax.ppermute(value, axis, [(i, (i + step) % count) for i in range(count)])  42.2 us
    ppermute x19, starting transfers between devices, neighbour(): lax.ppermute(value, axis, [(i, (i + step) % count) for i in range(count)])  36.8 us
    all_to_all x1, blocking collectives, window(): told = lax.all_to_all(slots, ('gx', 'st'), 0, 0, tiled=True)  24.1 us
    pallas_call x1, Pallas kernels, window(): call(backward_kernel, [mine, mine, (count, 2, DEPTH)], [vmem(big, f32)] *...  10.5 us
    pallas_call x1, Pallas kernels, window(): call(forward_kernel, [(3, WIDE, 4, WIDE, DEPTH), (OWN, 6, OWN, DEPTH), (O...  6.69 us
    pallas_call x1, Pallas kernels, window(): call(tile_kernel, [tiles] * 3 + [(1, 1), mine], [vmem(mine, f32)] * 2 + [...  4.98 us
  transfers between devices with their start and end apart: 19, of which 8 were waited for; matrix products, arithmetic and copies ran while one was open for 4% of the time, Pallas kernels for 7%

profile of v3, /device:TPU:1, one launch (start us, length us, event | category | flops | bytes accessed | tf_op | source)
XLA Modules:
  0.0 137.5 jit_solution(8066420962168940924)
XLA Ops:
  0.6 0.0 copy-start.2
  0.7 1.1 copy-done.2
  1.8 1.8 %shard_map.111 = (f32[416,128]{1,0:T(8,128)S(1)}, f32[416,128]{1,0:T(8,128)S(1)}, f32[416,128]{1,0:T(8,128)}, f32[416,128]{1,0:T(8,128)S(1)}, f32[416,128]{1,0:T(8,128)S(1)}, /*index=5*/f32[416,128]{1,0:T(8,128)S(1)}) custom-call(s32[1]{0:T(128)} %bitcast.place, f32[26,64,128]{2,1,0:T(8,128)S(1)} %bitcast.13), custom_call_target="tpu_custom_call" | custom-call | tf_op jit(solution)/shard_map/pallas_call | solution.py:652
  3.6 4.3 %collective-permute-start.6 = (f32[416,128]{1,0:T(8,128)}, f32[416,128]{1,0:T(8,128)S(1)}, u32[]{:S(2)}, u32[]{:S(2)}) collective-permute-start(f32[416,128]{1,0:T(8,128)} %get-tuple-element.42), channel_id=1, source_target_pairs={{0,3},{1,4},{2,5},{3,6},{4,7},{5,0},{6,1},{7,2},{8,11},{9,12},{10,... | collective-permute-start | bytes 638984 | tf_op jit(solution)/shard_map/ppermute | solution.py:638
  7.9 2.5 %fusion.1 = (f32[26,8,4,128]{3,2,1,0:T(4,128)}, f32[26,8,4,128]{3,2,1,0:T(4,128)}) fusion(f32[26,8,8,128]{3,2,1,0:T(8,128)} %own.1), kind=kLoop, calls=%fused_computation.8 | loop fusion | bytes 1703936 | tf_op jit(solution)/shard_map/slice | solution.py:687
  10.4 0.8 compare_select_fusion
  11.2 0.1 reshape.62
  11.3 0.8 convert_bitcast_fusion
  12.1 0.0 copy-start.1
  12.1 0.8 gather_fusion
  12.9 0.1 reshape.61
  13.0 0.1 convert_element_type.21
  13.1 0.1 stack_broadcast_in_dim.2
  13.1 0.5 shard_map.112
  13.7 0.4 collective-permute-start.10
  14.1 1.3 collective-permute-start.4
  15.4 0.6 collective-permute-start.8
  16.0 1.6 %collective-permute-start.1 = (f32[26,8,4,128]{3,2,1,0:T(4,128)}, f32[26,8,4,128]{3,2,1,0:T(4,128)S(1)}, u32[]{:S(2)}, u32[]{:S(2)}) collective-permute-start(f32[26,8,4,128]{3,2,1,0:T(4,128)} %get-tuple-element.72), channel_id=1, source_target_pairs={{0,7},{1,0},{2,1},{3,2},{4,3},{5,4},{6,5},{7,6},{8,15},{9,8},{10,9... | collective-permute-start | bytes 1277960 | tf_op jit(solution)/shard_map/ppermute | solution.py:638
  17.6 0.1 fusion
  17.6 6.5 %collective-permute-done.8.b.refs_5_ = f32[416,128]{1,0:T(8,128)S(1)} collective-permute-done((f32[416,128]{1,0:T(8,128)S(1)}, f32[416,128]{1,0:T(8,128)S(1)}, u32[]{:S(2)}, u32[]{:S(2)}) %collective-permute-start.8) | collective-permute-done | bytes 213024 | tf_op jit(solution)/shard_map/ppermute | solution.py:638
  24.2 1.0 collective-permute-start.5
  25.1 2.4 %collective-permute-start.7 = (f32[416,128]{1,0:T(8,128)S(1)}, f32[416,128]{1,0:T(8,128)S(1)}, u32[]{:S(2)}, u32[]{:S(2)}) collective-permute-start(f32[416,128]{1,0:T(8,128)S(1)} %get-tuple-element.43), channel_id=1, source_target_pairs={{0,4},{1,5},{2,6},{3,7},{4,0},{5,1},{6,2},{7,3},{8,12},{9,13},{10,... | collective-permute-start | bytes 638984 | tf_op jit(solution)/shard_map/ppermute | solution.py:638
  27.5 0.2 shard_map.113
  27.7 1.3 collective-permute-start.11
  29.1 0.2 pad_maximum_fusion.1
  29.3 8.1 %collective-permute-start.3 = (f32[26,4,16,128]{3,2,1,0:T(8,128)S(1)}, f32[26,4,16,128]{3,2,1,0:T(8,128)S(1)}, u32[]{:S(2)}, u32[]{:S(2)}) collective-permute-start(f32[26,4,16,128]{3,2,1,0:T(8,128)S(1)} %pad_maximum_fusion.1), channel_id=1, source_target_pairs={{0,248},{8,0},{16,8},{24,16},{32,24},{40,32},{48,40},{56,48},{64,5... | collective-permute-start | bytes 2555912 | tf_op jit(solution)/shard_map/ppermute | solution.py:638
  37.4 0.2 pad_maximum_fusion
  37.6 0.1 collective-permute-start.2
  37.7 6.4 %collective-permute-start.12 = (f32[960,128]{1,0:T(8,128)S(1)}, f32[960,128]{1,0:T(8,128)S(1)}, u32[]{:S(2)}, u32[]{:S(2)}) collective-permute-start(f32[960,128]{1,0:T(8,128)S(1)} %get-tuple-element.48), channel_id=1, source_target_pairs={{0,248},{8,0},{16,8},{24,16},{32,24},{40,32},{48,40},{56,48},{64,5... | collective-permute-start | bytes 1474568 | tf_op jit(solution)/shard_map/ppermute | solution.py:638
  44.1 0.2 shard_map.114
  44.3 0.1 collective-permute-start.13
  44.3 2.1 %collective-permute-done.11.from_left.refs_8_ = f32[960,128]{1,0:T(8,128)S(1)} collective-permute-done((f32[960,128]{1,0:T(8,128)S(1)}, f32[960,128]{1,0:T(8,128)S(1)}, u32[]{:S(2)}, u32[]{:S(2)}) %collective-permute-start.11) | collective-permute-done | bytes 491552 | tf_op jit(solution)/shard_map/ppermute | solution.py:638
  46.4 2.7 %collective-permute-start.14 = (f32[832,128]{1,0:T(8,128)S(1)}, f32[832,128]{1,0:T(8,128)S(1)}, u32[]{:S(2)}, u32[]{:S(2)}) collective-permute-start(f32[832,128]{1,0:T(8,128)S(1)} %get-tuple-element.50), channel_id=1, source_target_pairs={{0,248},{8,0},{16,8},{24,16},{32,24},{40,32},{48,40},{56,48},{64,5... | collective-permute-start | bytes 1277960 | tf_op jit(solution)/shard_map/ppermute | solution.py:638
  49.1 17.6 %collective-permute-done.12.from_right.refs_9_ = f32[960,128]{1,0:T(8,128)S(1)} collective-permute-done((f32[960,128]{1,0:T(8,128)S(1)}, f32[960,128]{1,0:T(8,128)S(1)}, u32[]{:S(2)}, u32[]{:S(2)}) %collective-permute-start.12) | collective-permute-done | bytes 491552 | tf_op jit(solution)/shard_map/ppermute | solution.py:638
  66.7 1.3 shard_map.115
  68.0 5.8 %collective-permute-done.13.refs_10_ = f32[832,128]{1,0:T(8,128)S(1)} collective-permute-done((f32[832,128]{1,0:T(8,128)S(1)}, f32[832,128]{1,0:T(8,128)S(1)}, u32[]{:S(2)}, u32[]{:S(2)}) %collective-permute-start.13) | collective-permute-done | bytes 426016 | tf_op jit(solution)/shard_map/ppermute | solution.py:638
  73.8 1.8 %collective-permute-done.14.refs_11_ = f32[832,128]{1,0:T(8,128)S(1)} collective-permute-done((f32[832,128]{1,0:T(8,128)S(1)}, f32[832,128]{1,0:T(8,128)S(1)}, u32[]{:S(2)}, u32[]{:S(2)}) %collective-permute-start.14) | collective-permute-done | bytes 426016 | tf_op jit(solution)/shard_map/ppermute | solution.py:638
  75.6 6.7 %shard_map.116 = (f32[3,16,4,16,128]{4,3,2,1,0:T(8,128)S(1)}, f32[8,6,8,128]{3,2,1,0:T(8,128)S(1)}, f32[8,6,4,128]{3,2,1,0:T(4,128)S(1)}, f32[8,6,4,128]{3,2,1,0:T(4,128)S(1)}, f32[1,128]{1,0:T(1,128)S(1)}) custom-call(s32[1]{0:T(128)} %bitcast.place, f32[416,128]{1,0:T(8,128)S(1)} %get-tuple-element.37.a.refs_0_, ...), custom_call_target="tpu_custom_call" | custom-call | tf_op jit(solution)/shard_map/pallas_call | solution.py:696
  82.3 0.7 collective-permute-start.15
  83.0 1.6 %collective-permute-done.15.lo.refs_1_ = f32[8,6,4,128]{3,2,1,0:T(4,128)S(1)} collective-permute-done((f32[8,6,4,128]{3,2,1,0:T(4,128)S(1)}, f32[8,6,4,128]{3,2,1,0:T(4,128)S(1)}, u32[]{:S(2)}, u32[]{:S(2)}) %collective-permute-start.15) | collective-permute-done | bytes 98336 | tf_op jit(solution)/shard_map/ppermute | solution.py:638
  84.6 2.7 %collective-permute-done.16.hi.refs_3_ = f32[8,6,4,128]{3,2,1,0:T(4,128)S(1)} collective-permute-done((f32[8,6,4,128]{3,2,1,0:T(4,128)S(1)}, f32[8,6,4,128]{3,2,1,0:T(4,128)S(1)}, u32[]{:S(2)}, u32[]{:S(2)}) %collective-permute-start.16) | collective-permute-done | bytes 98336 | tf_op jit(solution)/shard_map/ppermute | solution.py:638
  87.4 0.1 collective-permute-start.17
  87.4 5.8 %collective-permute-start.18 = (f32[4,6,16,128]{3,2,1,0:T(8,128)S(1)}, f32[4,6,16,128]{3,2,1,0:T(8,128)S(1)}, u32[]{:S(2)}, u32[]{:S(2)}) collective-permute-start(f32[4,6,16,128]{3,2,1,0:T(8,128)S(1)} %get-tuple-element.57), channel_id=1, source_target_pairs={{0,248},{8,0},{16,8},{24,16},{32,24},{40,32},{48,40},{56,48},{64,5... | collective-permute-start | bytes 589832 | tf_op jit(solution)/shard_map/ppermute | solution.py:638
  93.2 0.5 shard_map.110.refs_0_
  93.7 4.1 %collective-permute-done.17.refs_4_ = f32[4,6,16,128]{3,2,1,0:T(8,128)S(1)} collective-permute-done((f32[4,6,16,128]{3,2,1,0:T(8,128)S(1)}, f32[4,6,16,128]{3,2,1,0:T(8,128)S(1)}, u32[]{:S(2)}, u32[]{:S(2)}) %collective-permute-start.17) | collective-permute-done | bytes 196640 | tf_op jit(solution)/shard_map/ppermute | solution.py:638
  97.8 10.5 %shard_map.118 = (f32[26,8,8,128]{3,2,1,0:T(8,128)S(1)}, f32[26,8,8,128]{3,2,1,0:T(8,128)S(1)}, f32[256,2,128]{2,1,0:T(2,128)S(1)}) custom-call(f32[16,26,16,128]{3,2,1,0:T(8,128)S(1)} %shard_map.110.refs_0_, f32[8,6,4,128]{3,2,1,0:T(4,128)S(1)} %collective-permute-done.15.lo.refs_1_, f32[8,6,8,128]{3,2,1,0:T(8,128)S(1)} %get-tuple-element.54.mid.refs_2_, ...), custom_call_target="tpu_custom_call" | custom-call | tf_op jit(solution)/shard_map/pallas_call | solution.py:712
  108.2 24.1 %all_to_all.5 = f32[256,2,128]{2,1,0:T(2,128)S(1)} all-to-all(f32[256,2,128]{2,1,0:T(2,128)S(1)} %get-tuple-element.61), channel_id=1, replica_groups=mesh['gx'=32,'st'=8] {'gx','st'}, dimensions={0} | all-to-all | bytes 524288 | tf_op jit(solution)/shard_map/all_to_all | solution.py:722
  132.4 5.0 %shard_map.119 = (f32[32,128]{1,0:T(8,128)}, f32[32,128]{1,0:T(8,128)}, f32[32,128]{1,0:T(8,128)}, f32[1,1]{1,0:T(1,128)}, f32[26,8,8,128]{3,2,1,0:T(8,128)}) custom-call(f32[1]{0:T(128)} %constant.5.clone.1.scale, f32[512,128]{1,0:T(8,128)S(1)} %bitcast.15, f32[32,128]{1,0:T(8,128)S(1)} %bitcast.12, f32[32,128]{1,0:T(8,128)S(1)} %bitcast.16, ...), custom_call_target="tpu_custom_call" | custom-call | tf_op jit(solution)/shard_map/pallas_call | solution.py:726
  (32 shorter events, 0.2 us)
Async XLA Ops:
  0.6 11.5 %copy-start = (f32[4096]{0:T(1024)S(1)}, f32[4096]{0:T(1024)}, u32[]{:S(2)}) copy-start(f32[4096]{0:T(1024)} %param.11) | copy-start | bytes 49156
  0.6 1.2 copy-start.2
  1.8 10.3 %copy-start.6 = (s32[8,8]{1,0:T(8,128)S(1)}, s32[8,8]{1,0:T(8,128)}, u32[]{:S(2)}) copy-start(s32[8,8]{1,0:T(8,128)} %param.10) | copy-start | bytes 772
  3.6 12.4 %collective-permute-start.6 = (f32[416,128]{1,0:T(8,128)}, f32[416,128]{1,0:T(8,128)S(1)}, u32[]{:S(2)}, u32[]{:S(2)}) collective-permute-start(f32[416,128]{1,0:T(8,128)} %get-tuple-element.42), channel_id=1, source_target_pairs={{0,3},{1,4},{2,5},{3,6},{4,7},{5,0},{6,1},{7,2},{8,11},{9,12},{10,... | collective-permute-start | bytes 638984 | tf_op jit(solution)/shard_map/ppermute | solution.py:638
  10.4 2.7 %copy-start.3 = (f32[26,1,64,128]{3,2,1,0:T(8,128)S(1)}, f32[26,1,64,128]{3,2,1,0:T(8,128)}, u32[]{:S(2)}) copy-start(f32[26,1,64,128]{3,2,1,0:T(8,128)} %param.7) | copy-start | bytes 2555908
  10.4 17.3 %collective-permute-start = (f32[26,8,4,128]{3,2,1,0:T(4,128)}, f32[26,8,4,128]{3,2,1,0:T(4,128)S(1)}, u32[]{:S(2)}, u32[]{:S(2)}) collective-permute-start(f32[26,8,4,128]{3,2,1,0:T(4,128)} %get-tuple-element.71), channel_id=1, source_target_pairs={{0,1},{1,2},{2,3},{3,4},{4,5},{5,6},{6,7},{7,0},{8,9},{9,10},{10,1... | collective-permute-start | bytes 1277960 | tf_op jit(solution)/shard_map/ppermute | solution.py:638
  12.1 5.5 %copy-start.1 = (f32[26,8,8,128]{3,2,1,0:T(8,128)S(1)}, f32[26,8,8,128]{3,2,1,0:T(8,128)}, u32[]{:S(2)}) copy-start(f32[26,8,8,128]{3,2,1,0:T(8,128)} %own.1) | copy-start | bytes 2555908
  13.7 11.5 %collective-permute-start.10 = (f32[480,128]{1,0:T(8,128)S(1)}, f32[480,128]{1,0:T(8,128)S(1)}, u32[]{:S(2)}, u32[]{:S(2)}) collective-permute-start(f32[480,128]{1,0:T(8,128)S(1)} %get-tuple-element.46), channel_id=1, source_target_pairs={{0,7},{1,0},{2,1},{3,2},{4,3},{5,4},{6,5},{7,6},{8,15},{9,8},{10,9... | collective-permute-start | bytes 737288 | tf_op jit(solution)/shard_map/ppermute | solution.py:638
  14.1 13.4 %collective-permute-start.4 = (f32[480,128]{1,0:T(8,128)S(1)}, f32[480,128]{1,0:T(8,128)S(1)}, u32[]{:S(2)}, u32[]{:S(2)}) collective-permute-start(f32[480,128]{1,0:T(8,128)S(1)} %get-tuple-element.40), channel_id=1, source_target_pairs={{0,1},{1,2},{2,3},{3,4},{4,5},{5,6},{6,7},{7,0},{8,9},{9,10},{10,1... | collective-permute-start | bytes 737288 | tf_op jit(solution)/shard_map/ppermute | solution.py:638
  15.4 8.7 %collective-permute-start.8 = (f32[416,128]{1,0:T(8,128)S(1)}, f32[416,128]{1,0:T(8,128)S(1)}, u32[]{:S(2)}, u32[]{:S(2)}) collective-permute-start(f32[416,128]{1,0:T(8,128)S(1)} %get-tuple-element.44), channel_id=1, source_target_pairs={{0,5},{1,6},{2,7},{3,0},{4,1},{5,2},{6,3},{7,4},{8,13},{9,14},{10,... | collective-permute-start | bytes 638984 | tf_op jit(solution)/shard_map/ppermute | solution.py:638
  16.0 13.1 %collective-permute-start.1 = (f32[26,8,4,128]{3,2,1,0:T(4,128)}, f32[26,8,4,128]{3,2,1,0:T(4,128)S(1)}, u32[]{:S(2)}, u32[]{:S(2)}) collective-permute-start(f32[26,8,4,128]{3,2,1,0:T(4,128)} %get-tuple-element.72), channel_id=1, source_target_pairs={{0,7},{1,0},{2,1},{3,2},{4,3},{5,4},{6,5},{7,6},{8,15},{9,8},{10,9... | collective-permute-start | bytes 1277960 | tf_op jit(solution)/shard_map/ppermute | solution.py:638
  24.2 13.4 %collective-permute-start.5 = (f32[416,128]{1,0:T(8,128)S(1)}, f32[416,128]{1,0:T(8,128)S(1)}, u32[]{:S(2)}, u32[]{:S(2)}) collective-permute-start(f32[416,128]{1,0:T(8,128)S(1)} %get-tuple-element.41), channel_id=1, source_target_pairs={{0,2},{1,3},{2,4},{3,5},{4,6},{5,7},{6,0},{7,1},{8,10},{9,11},{10,... | collective-permute-start | bytes 638984 | tf_op jit(solution)/shard_map/ppermute | solution.py:638
  25.1 12.5 %collective-permute-start.7 = (f32[416,128]{1,0:T(8,128)S(1)}, f32[416,128]{1,0:T(8,128)S(1)}, u32[]{:S(2)}, u32[]{:S(2)}) collective-permute-start(f32[416,128]{1,0:T(8,128)S(1)} %get-tuple-element.43), channel_id=1, source_target_pairs={{0,4},{1,5},{2,6},{3,7},{4,0},{5,1},{6,2},{7,3},{8,12},{9,13},{10,... | collective-permute-start | bytes 638984 | tf_op jit(solution)/shard_map/ppermute | solution.py:638
  27.5 16.5 %collective-permute-start.9 = (f32[416,128]{1,0:T(8,128)S(1)}, f32[416,128]{1,0:T(8,128)S(1)}, u32[]{:S(2)}, u32[]{:S(2)}) collective-permute-start(f32[416,128]{1,0:T(8,128)S(1)} %get-tuple-element.45), channel_id=1, source_target_pairs={{0,6},{1,7},{2,0},{3,1},{4,2},{5,3},{6,4},{7,5},{8,14},{9,15},{10,... | collective-permute-start | bytes 638984 | tf_op jit(solution)/shard_map/ppermute | solution.py:638
  27.7 18.7 %collective-permute-start.11 = (f32[960,128]{1,0:T(8,128)S(1)}, f32[960,128]{1,0:T(8,128)S(1)}, u32[]{:S(2)}, u32[]{:S(2)}) collective-permute-start(f32[960,128]{1,0:T(8,128)S(1)} %get-tuple-element.47), channel_id=1, source_target_pairs={{0,8},{8,16},{16,24},{24,32},{32,40},{40,48},{48,56},{56,64},{64,7... | collective-permute-start | bytes 1474568 | tf_op jit(solution)/shard_map/ppermute | solution.py:638
  29.3 63.9 %collective-permute-start.3 = (f32[26,4,16,128]{3,2,1,0:T(8,128)S(1)}, f32[26,4,16,128]{3,2,1,0:T(8,128)S(1)}, u32[]{:S(2)}, u32[]{:S(2)}) collective-permute-start(f32[26,4,16,128]{3,2,1,0:T(8,128)S(1)} %pad_maximum_fusion.1), channel_id=1, source_target_pairs={{0,248},{8,0},{16,8},{24,16},{32,24},{40,32},{48,40},{56,48},{64,5... | collective-permute-start | bytes 2555912 | tf_op jit(solution)/shard_map/ppermute | solution.py:638
  37.6 55.7 %collective-permute-start.2 = (f32[26,4,16,128]{3,2,1,0:T(8,128)S(1)}, f32[26,4,16,128]{3,2,1,0:T(8,128)S(1)}, u32[]{:S(2)}, u32[]{:S(2)}) collective-permute-start(f32[26,4,16,128]{3,2,1,0:T(8,128)S(1)} %pad_maximum_fusion), channel_id=1, source_target_pairs={{0,8},{8,16},{16,24},{24,32},{32,40},{40,48},{48,56},{56,64},{64,7... | collective-permute-start | bytes 2555912 | tf_op jit(solution)/shard_map/ppermute | solution.py:638
  37.7 29.0 %collective-permute-start.12 = (f32[960,128]{1,0:T(8,128)S(1)}, f32[960,128]{1,0:T(8,128)S(1)}, u32[]{:S(2)}, u32[]{:S(2)}) collective-permute-start(f32[960,128]{1,0:T(8,128)S(1)} %get-tuple-element.48), channel_id=1, source_target_pairs={{0,248},{8,0},{16,8},{24,16},{32,24},{40,32},{48,40},{56,48},{64,5... | collective-permute-start | bytes 1474568 | tf_op jit(solution)/shard_map/ppermute | solution.py:638
  44.3 29.5 %collective-permute-start.13 = (f32[832,128]{1,0:T(8,128)S(1)}, f32[832,128]{1,0:T(8,128)S(1)}, u32[]{:S(2)}, u32[]{:S(2)}) collective-permute-start(f32[832,128]{1,0:T(8,128)S(1)} %get-tuple-element.49), channel_id=1, source_target_pairs={{0,8},{8,16},{16,24},{24,32},{32,40},{40,48},{48,56},{56,64},{64,7... | collective-permute-start | bytes 1277960 | tf_op jit(solution)/shard_map/ppermute | solution.py:638
  46.4 29.2 %collective-permute-start.14 = (f32[832,128]{1,0:T(8,128)S(1)}, f32[832,128]{1,0:T(8,128)S(1)}, u32[]{:S(2)}, u32[]{:S(2)}) collective-permute-start(f32[832,128]{1,0:T(8,128)S(1)} %get-tuple-element.50), channel_id=1, source_target_pairs={{0,248},{8,0},{16,8},{24,16},{32,24},{40,32},{48,40},{56,48},{64,5... | collective-permute-start | bytes 1277960 | tf_op jit(solution)/shard_map/ppermute | solution.py:638
  82.3 2.3 %collective-permute-start.15 = (f32[8,6,4,128]{3,2,1,0:T(4,128)S(1)}, f32[8,6,4,128]{3,2,1,0:T(4,128)S(1)}, u32[]{:S(2)}, u32[]{:S(2)}) collective-permute-start(f32[8,6,4,128]{3,2,1,0:T(4,128)S(1)} %get-tuple-element.53), channel_id=1, source_target_pairs={{0,1},{1,2},{2,3},{3,4},{4,5},{5,6},{6,7},{7,0},{8,9},{9,10},{10,1... | collective-permute-start | bytes 294920 | tf_op jit(solution)/shard_map/ppermute | solution.py:638
  83.0 4.3 %collective-permute-start.16 = (f32[8,6,4,128]{3,2,1,0:T(4,128)S(1)}, f32[8,6,4,128]{3,2,1,0:T(4,128)S(1)}, u32[]{:S(2)}, u32[]{:S(2)}) collective-permute-start(f32[8,6,4,128]{3,2,1,0:T(4,128)S(1)} %get-tuple-element.55), channel_id=1, source_target_pairs={{0,7},{1,0},{2,1},{3,2},{4,3},{5,4},{6,5},{7,6},{8,15},{9,8},{10,9... | collective-permute-start | bytes 294920 | tf_op jit(solution)/shard_map/ppermute | solution.py:638
  87.4 10.4 %collective-permute-start.17 = (f32[4,6,16,128]{3,2,1,0:T(8,128)S(1)}, f32[4,6,16,128]{3,2,1,0:T(8,128)S(1)}, u32[]{:S(2)}, u32[]{:S(2)}) collective-permute-start(f32[4,6,16,128]{3,2,1,0:T(8,128)S(1)} %get-tuple-element.56), channel_id=1, source_target_pairs={{0,8},{8,16},{16,24},{24,32},{32,40},{40,48},{48,56},{56,64},{64,7... | collective-permute-start | bytes 589832 | tf_op jit(solution)/shard_map/ppermute | solution.py:638
  87.4 10.3 %collective-permute-start.18 = (f32[4,6,16,128]{3,2,1,0:T(8,128)S(1)}, f32[4,6,16,128]{3,2,1,0:T(8,128)S(1)}, u32[]{:S(2)}, u32[]{:S(2)}) collective-permute-start(f32[4,6,16,128]{3,2,1,0:T(8,128)S(1)} %get-tuple-element.57), channel_id=1, source_target_pairs={{0,248},{8,0},{16,8},{24,16},{32,24},{40,32},{48,40},{56,48},{64,5... | collective-permute-start | bytes 589832 | tf_op jit(solution)/shard_map/ppermute | solution.py:638
  97.8 34.6 %copy-start.4 = (f32[4096]{0:T(1024)S(1)}, f32[4096]{0:T(1024)}, u32[]{:S(2)}) copy-start(f32[4096]{0:T(1024)} %param.12) | copy-start | bytes 49156
  97.8 34.6 %copy-start.5 = (f32[4096]{0:T(1024)S(1)}, f32[4096]{0:T(1024)}, u32[]{:S(2)}) copy-start(f32[4096]{0:T(1024)} %param.13) | copy-start | bytes 49156
